TPU v7x, 32 devices: a whole 2x2x4 slice. The times are simulated.
32 devices in a mesh: groups: 2 (over x), view: 16 (over z, y, core).
Axes of the slice: x: 2, y: 2, z: 4, core: 2. Of those that a mesh axis runs over, the one named last changes fastest.
Arguments:
- ref_features: bfloat16 [256, 32, 384], P(('groups', 'view')), parts along dimension 0, may hold values from -6 to 6
- source_tiles: bfloat16 [1024, 2, 32, 384], P(('groups', 'view')), parts along dimension 0, may hold values from -6 to 6
- pair_lists: int32 [32, 4, 4], P(('groups', 'view')), parts along dimension 0, may hold values from -1 to 511, as said below
- view_counts: int32 [32], P(('groups', 'view')), parts along dimension 0, may hold values from 3 to 4, as said below
- disparities: int32 [16, 4], P('groups'), parts along dimension 0, may hold values from -48 to 48
- conv_first: bfloat16 [3, 3, 8, 3, 32], replicated, may hold values from -0.21875 to 0.21875
- bias_first: float32 [8], replicated, may hold values from -3 to 3
- conv_second: bfloat16 [16, 3, 3, 3, 8], replicated, may hold values from -0.4375 to 0.4375
- bias_second: float32 [16], replicated, may hold values from -3 to 3
Outputs:
- cost_features: float32 [8, 64, 16, 192], P('groups', 'view'), parts along dimension 0
There are 2 independent parts, one for each index of `groups`. A program takes and returns all parts, laid end to end along the dimension named above; an argument that names none is the same for every part. Nothing has to cross between parts.
Inputs may be any that keep to these rules, and one draw needn't show every extreme that they name: pair_lists[v, s, b] is the tile holding rows 2b and 2b + 1 of source s of strip v; it is -1 exactly when s >= view_counts[v]; tile t lies on device t // 32 of the view axis; no strip takes more than 2 tiles from one device, and some strip takes exactly 2 from some device. `view_counts`: some strip uses 3 sources and some uses 4.
All inputs are finite; a program needn't handle non-finite values.
Results may differ from a plain program's by a relative error of at most 0.0028.
Values may be sent and summed in bfloat16 or wider, within the bound.
A program may use at most 128 MiB of HBM per device.

v0:
```python
import jax
import jax.numpy as jnp
from jax import lax
from jax.sharding import PartitionSpec as P

C = 32
C1 = 8
C2 = 16
PLANES = 8
SOURCES = 4
SHIFT = 48
TILES_DEV = 32


def with_halo(x, sides, width):
    for axis, dim in sides:
        count, length = (lax.axis_size(axis), x.shape[dim])
        up = [(i, (i + 1) % count) for i in range(count - 1)]
        down = [(j, i) for i, j in up]
        last = lax.slice_in_dim(x, length - width, length, axis=dim)
        initial = lax.slice_in_dim(x, 0, width, axis=dim)
        before = lax.ppermute(last, axis, up)
        after = lax.ppermute(initial, axis, down)
        x = jnp.concatenate([before, x, after], axis=dim)
    return x


def passed_along(x, axis, by):
    count = lax.axis_size(axis)
    pairs = [(i, i + by) for i in range(count) if 0 <= i + by < count]
    return lax.ppermute(x, axis, pairs)


def shifted(rows, offset):
    padded = jnp.pad(rows, ((0, 0), (0, 0), (SHIFT, SHIFT)))
    return lax.dynamic_slice_in_dim(padded, SHIFT - offset, rows.shape[2], 2)


def request_slots(flat_ids, slot_cap):
    is_live = flat_ids >= 0
    owners = jnp.where(is_live, flat_ids // TILES_DEV, -1)
    count_req = flat_ids.shape[0]
    earlier = jnp.arange(count_req)[None, :] < jnp.arange(count_req)[:, None]
    same_owner = (owners[:, None] == owners[None, :]) & earlier & is_live[None, :]
    slot_rank = jnp.sum(same_owner.astype(jnp.int32), axis=1)
    slot_ids = jnp.where(is_live, owners * slot_cap + slot_rank, -1)
    return (slot_ids, flat_ids % TILES_DEV)


def request_table(slot_ids, local_ids, n_view, slot_cap):
    positions = jnp.arange(n_view * slot_cap)
    matches = slot_ids[:, None] == positions[None, :]
    wanted = jnp.sum(jnp.where(matches, local_ids[:, None] + 1, 0), axis=0) - 1
    return wanted.reshape(n_view, slot_cap)


def first_conv(rows_in, conv_first):
    planes, rows_n, channels, n_cols = rows_in.shape
    kernel = conv_first.reshape(9 * C1, 3 * channels)
    padded = jnp.pad(rows_in, ((1, 1), (0, 0), (0, 0), (1, 1)))
    columns = jnp.concatenate(
        [padded[:, :, :, col_tap : col_tap + n_cols] for col_tap in range(3)], axis=2
    )
    block_planes = min(8, planes)
    tap_out = jnp.einsum("oc,prcx->prox", kernel, columns, preferred_element_type=jnp.float32)
    tap_out = tap_out.reshape(block_planes + 2, rows_n, 3, 3, C1, n_cols)
    partial_sum = jnp.zeros((block_planes, rows_n - 2, C1, n_cols), jnp.float32)
    for plane_tap in range(3):
        for row_tap in range(3):
            partial_sum = (
                partial_sum
                + tap_out[
                    plane_tap : plane_tap + block_planes,
                    row_tap : row_tap + rows_n - 2,
                    plane_tap,
                    row_tap,
                ]
            )
    return partial_sum


def on_device(
    ref_features,
    source_tiles,
    pair_lists,
    view_counts,
    disparities,
    conv_first,
    bias_first,
    conv_second,
    bias_second,
):
    n_view = lax.axis_size("view")
    rows_n = ref_features.shape[0]
    n_cols = ref_features.shape[2]
    request_total = SOURCES * (rows_n // 2)
    slot_cap = max(2, (request_total + n_view - 1) // n_view)
    flat_ids = pair_lists.reshape(request_total)
    slot_ids, local_ids = request_slots(flat_ids, slot_cap)
    wanted = request_table(slot_ids, local_ids, n_view, slot_cap)
    outgoing = source_tiles[
        jnp.maximum(lax.all_to_all(wanted, "view", split_axis=0, concat_axis=0, tiled=True), 0)
    ]
    arrived = lax.all_to_all(outgoing, "view", split_axis=0, concat_axis=0, tiled=True)
    picked = arrived.reshape(n_view * slot_cap, 2, C, n_cols)[jnp.maximum(slot_ids, 0)]
    picked = picked.reshape(SOURCES, rows_n, C, n_cols)
    live_count = view_counts[0]
    ref_wide = ref_features.astype(jnp.float32)
    summed = jnp.broadcast_to(ref_wide, (PLANES,) + ref_wide.shape)
    squares = summed * summed
    for source in range(SOURCES):
        warped = jax.vmap(lambda offset: shifted(picked[source], offset))(
            disparities[:, source]
        ).astype(jnp.float32)
        weight = (source < live_count).astype(jnp.float32)
        summed = summed + weight * warped
        squares = squares + weight * warped * warped
    view_total = live_count.astype(jnp.float32) + 1.0
    view_mean = summed / view_total
    volume = (squares / view_total - view_mean * view_mean).astype(jnp.bfloat16)
    widened = with_halo(volume, (("view", 1),), 1)
    interior = first_conv(widened, conv_first)
    cost_first = jnp.maximum(interior + bias_first[None, None, :, None], 0.0).astype(jnp.bfloat16)
    upper_rim = passed_along(cost_first[:, rows_n - 1 : rows_n], "view", 1)
    stacked = jnp.concatenate([upper_rim, cost_first], axis=1)
    padded = jnp.pad(stacked, ((1, 0), (0, 0), (0, 0), (1, 0)))
    half_p = PLANES // 2
    half_r = rows_n // 2
    half_x = n_cols // 2
    tap_list = []
    for plane_tap in range(3):
        for row_tap in range(3):
            for col_tap in range(3):
                tap_list.append(
                    padded[
                        plane_tap : plane_tap + 2 * half_p : 2,
                        row_tap : row_tap + 2 * half_r : 2,
                        :,
                        col_tap : col_tap + 2 * half_x : 2,
                    ]
                )
    gathered = jnp.concatenate(tap_list, axis=2)
    kernel_two = conv_second.reshape(C2, 27 * C1)
    result = jnp.einsum("oc,prcx->prox", kernel_two, gathered, preferred_element_type=jnp.float32)
    return result + bias_second[None, None, :, None]


def solution(mesh):
    return jax.shard_map(
        on_device,
        mesh=mesh,
        in_specs=(
            P(("groups", "view"), None, None),
            P(("groups", "view"), None, None, None),
            P(("groups", "view"), None, None),
            P(("groups", "view")),
            P("groups", None),
            P(),
            P(),
            P(),
            P(),
        ),
        out_specs=P("groups", "view", None, None),
        check_vma=False,
    )
```

profile of v0, /device:TPU:16, one launch (start us, length us, event | category | flops | bytes accessed | tf_op | source)
XLA Modules:
  0.0 426.3 jit_solution(14030624873482726831)
XLA Ops:
  0.0 0.9 reshape.260
  1.3 10.1 %all_to_all.11 = s32[16,1,2]{2,1,0:T(1,128)S(1)} all-to-all(s32[16,1,2]{2,1,0:T(1,128)S(1)} %bitcast.112), channel_id=1, replica_groups=mesh['groups'=2,'view'=16] {'view'}, dimensions={0} | all-to-all | bytes 256 | tf_op jit(solution)/shard_map/all_to_all | solution.py:102
  11.6 1.9 gather_fusion
  13.5 5.9 %all-to-all-start.1 = ((bf16[16,2,2,32,384]{4,3,2,1,0:T(8,128)(2,1)}), bf16[16,2,2,32,384]{4,3,2,1,0:T(8,128)(2,1)S(1)}, u32[]{:S(2)}, u32[]{:S(2)}) async-start(bf16[16,2,2,32,384]{4,3,2,1,0:T(8,128)(2,1)} %bitcast.2), calls=%async_computation.1 | async-start | bytes 3145728 | tf_op jit(solution)/shard_map/all_to_all | solution.py:104
  20.2 0.8 convert_element_type.61
  21.1 0.8 convert_multiply_fusion
  21.9 33.9 %all-to-all-done.1 = bf16[16,2,2,32,384]{4,3,2,1,0:T(8,128)(2,1)S(1)} async-done(((bf16[16,2,2,32,384]{4,3,2,1,0:T(8,128)(2,1)}), bf16[16,2,2,32,384]{4,3,2,1,0:T(8,128)(2,1)S(1)}, u32[]{:S(2)}, u32[]{:S(2)}) %all-to-all-start.1) | async-done | bytes 1572896 | tf_op jit(solution)/shard_map/all_to_all | solution.py:104
  55.8 0.7 gather_fusion.1
  56.6 0.5 copy.69
  57.1 0.5 copy.65
  58.0 1.3 copy.67
  59.3 1.3 pad.26
  60.6 1.3 copy.71
  62.0 2.3 pad.28
  64.2 5.2 %gather_fusion.5 = bf16[8,8,32,384]{2,1,3,0:T(8,128)(2,1)} fusion(bf16[8,32,480]{1,0,2:T(8,128)(2,1)} %pad.28, s32[8]{0:T(128)S(1)} %get-tuple-element.16), kind=kCustom, calls=%fused_computation.5 | custom fusion | bytes 3145824 | tf_op jit(solution)/shard_map/vmap()/gather | solution.py:36
  69.4 6.8 %copy.72 = bf16[8,8,32,384]{3,2,1,0:T(8,128)(2,1)} copy(bf16[8,8,32,384]{2,1,3,0:T(8,128)(2,1)} %gather_fusion.5) | data formatting | bytes 3145728 | tf_op jit(solution)/shard_map/vmap()/gather | solution.py:36
  76.2 4.0 gather_fusion.3
  80.2 6.8 %copy.68 = bf16[8,8,32,384]{3,2,1,0:T(8,128)(2,1)} copy(bf16[8,8,32,384]{2,1,3,0:T(8,128)(2,1)} %gather_fusion.3) | data formatting | bytes 3145728 | tf_op jit(solution)/shard_map/vmap()/gather | solution.py:36
  87.0 4.0 gather_fusion.2
  91.0 6.8 %copy.66 = bf16[8,8,32,384]{3,2,1,0:T(8,128)(2,1)} copy(bf16[8,8,32,384]{2,1,3,0:T(8,128)(2,1)} %gather_fusion.2) | data formatting | bytes 3145728 | tf_op jit(solution)/shard_map/vmap()/gather | solution.py:36
  97.8 4.0 gather_fusion.4
  101.8 6.9 %copy.70 = bf16[8,8,32,384]{3,2,1,0:T(8,128)(2,1)} copy(bf16[8,8,32,384]{2,1,3,0:T(8,128)(2,1)} %gather_fusion.4) | data formatting | bytes 3145728 | tf_op jit(solution)/shard_map/vmap()/gather | solution.py:36
  108.8 4.2 fusion.20
  113.1 1.9 collective-permute-start
  115.0 4.7 %collective-permute-start.1 = (bf16[8,1,32,384]{3,2,1,0:T(8,128)(2,1)S(1)}, bf16[8,1,32,384]{3,2,1,0:T(8,128)(2,1)S(1)}, u32[]{:S(2)}, u32[]{:S(2)}) collective-permute-start(bf16[8,1,32,384]{3,2,1,0:T(8,128)(2,1)S(1)} %get-tuple-element.9), channel_id=1, source_target_pairs={{1,0},{2,1},{3,2},{4,3},{5,4},{6,5},{7,6},{8,7},{9,8},{10,9},{11,1... | collective-permute-start | bytes 589832 | tf_op jit(solution)/shard_map/ppermute | solution.py:23
  119.9 1.2 collective-permute-done
  121.1 1.7 collective-permute-done.1
  122.7 1.8 select_maximum_fusion
  124.5 2.0 fusion.46
  126.5 2.4 fusion
  128.9 0.3 fusion.26
  129.3 2.1 collective-permute-start.2
  131.4 4.4 %collective-permute-done.2 = bf16[8,1,8,384]{3,2,1,0:T(8,128)(2,1)S(1)} collective-permute-done((bf16[8,1,8,384]{3,2,1,0:T(8,128)(2,1)S(1)}, bf16[8,1,8,384]{3,2,1,0:T(8,128)(2,1)S(1)}, u32[]{:S(2)}, u32[]{:S(2)}) %collective-permute-start.2) | collective-permute-done | bytes 49184 | tf_op jit(solution)/shard_map/ppermute | solution.py:31
  135.8 4.8 %copy.83 = bf16[8,9,8,384]{2,3,1,0:T(8,128)(2,1)} copy(bf16[8,9,8,384]{3,2,1,0:T(8,128)(2,1)S(1)} %pad_maximum_fusion) | data formatting | bytes 884736 | tf_op jit(solution)/shard_map/concatenate | solution.py:125
  140.6 9.0 %pad.30 = bf16[9,9,8,385]{2,3,1,0:T(8,128)(2,1)} pad(bf16[8,9,8,384]{2,3,1,0:T(8,128)(2,1)} %copy.83, bf16[]{:T(256)} %constant.61.clone.1), padding=1_0x0_0x0_0x1_0 | pad | bytes 941330 | tf_op jit(solution)/shard_map/jit(_pad)/pad | solution.py:126
  149.6 9.5 %slice.203 = bf16[4,4,8,192]{2,3,1,0:T(8,128)(2,1)} slice(bf16[9,9,8,385]{2,3,1,0:T(8,128)(2,1)} %pad.30), slice={[2:9:2], [2:9:2], [0:8:1], [2:385:2]} | slice | bytes 98304 | tf_op jit(solution)/shard_map/slice | solution.py:135
  159.0 9.5 %slice.202 = bf16[4,4,8,192]{2,3,1,0:T(8,128)(2,1)} slice(bf16[9,9,8,385]{2,3,1,0:T(8,128)(2,1)} %pad.30), slice={[2:9:2], [2:9:2], [0:8:1], [1:385:2]} | slice | bytes 98304 | tf_op jit(solution)/shard_map/slice | solution.py:135
  168.5 9.5 %slice.201 = bf16[4,4,8,192]{2,3,1,0:T(8,128)(2,1)} slice(bf16[9,9,8,385]{2,3,1,0:T(8,128)(2,1)} %pad.30), slice={[2:9:2], [2:9:2], [0:8:1], [0:384:2]} | slice | bytes 98304 | tf_op jit(solution)/shard_map/slice | solution.py:135
  178.0 9.6 %slice.200 = bf16[4,4,8,192]{2,3,1,0:T(8,128)(2,1)} slice(bf16[9,9,8,385]{2,3,1,0:T(8,128)(2,1)} %pad.30), slice={[2:9:2], [1:9:2], [0:8:1], [2:385:2]} | slice | bytes 98304 | tf_op jit(solution)/shard_map/slice | solution.py:135
  187.6 9.6 %slice.199 = bf16[4,4,8,192]{2,3,1,0:T(8,128)(2,1)} slice(bf16[9,9,8,385]{2,3,1,0:T(8,128)(2,1)} %pad.30), slice={[2:9:2], [1:9:2], [0:8:1], [1:385:2]} | slice | bytes 98304 | tf_op jit(solution)/shard_map/slice | solution.py:135
  197.2 9.5 %slice.198 = bf16[4,4,8,192]{2,3,1,0:T(8,128)(2,1)} slice(bf16[9,9,8,385]{2,3,1,0:T(8,128)(2,1)} %pad.30), slice={[2:9:2], [1:9:2], [0:8:1], [0:384:2]} | slice | bytes 98304 | tf_op jit(solution)/shard_map/slice | solution.py:135
  206.7 9.6 %slice.197 = bf16[4,4,8,192]{2,3,1,0:T(8,128)(2,1)} slice(bf16[9,9,8,385]{2,3,1,0:T(8,128)(2,1)} %pad.30), slice={[2:9:2], [0:8:2], [0:8:1], [2:385:2]} | slice | bytes 98304 | tf_op jit(solution)/shard_map/slice | solution.py:135
  216.3 9.6 %slice.196 = bf16[4,4,8,192]{2,3,1,0:T(8,128)(2,1)} slice(bf16[9,9,8,385]{2,3,1,0:T(8,128)(2,1)} %pad.30), slice={[2:9:2], [0:8:2], [0:8:1], [1:385:2]} | slice | bytes 98304 | tf_op jit(solution)/shard_map/slice | solution.py:135
  225.8 9.6 %slice.195 = bf16[4,4,8,192]{2,3,1,0:T(8,128)(2,1)} slice(bf16[9,9,8,385]{2,3,1,0:T(8,128)(2,1)} %pad.30), slice={[2:9:2], [0:8:2], [0:8:1], [0:384:2]} | slice | bytes 98304 | tf_op jit(solution)/shard_map/slice | solution.py:135
  235.4 9.5 %slice.194 = bf16[4,4,8,192]{2,3,1,0:T(8,128)(2,1)} slice(bf16[9,9,8,385]{2,3,1,0:T(8,128)(2,1)} %pad.30), slice={[1:9:2], [2:9:2], [0:8:1], [2:385:2]} | slice | bytes 98304 | tf_op jit(solution)/shard_map/slice | solution.py:135
  244.9 9.5 %slice.193 = bf16[4,4,8,192]{2,3,1,0:T(8,128)(2,1)} slice(bf16[9,9,8,385]{2,3,1,0:T(8,128)(2,1)} %pad.30), slice={[1:9:2], [2:9:2], [0:8:1], [1:385:2]} | slice | bytes 98304 | tf_op jit(solution)/shard_map/slice | solution.py:135
  254.4 9.5 %slice.192 = bf16[4,4,8,192]{2,3,1,0:T(8,128)(2,1)} slice(bf16[9,9,8,385]{2,3,1,0:T(8,128)(2,1)} %pad.30), slice={[1:9:2], [2:9:2], [0:8:1], [0:384:2]} | slice | bytes 98304 | tf_op jit(solution)/shard_map/slice | solution.py:135
  263.9 9.6 %slice.191 = bf16[4,4,8,192]{2,3,1,0:T(8,128)(2,1)} slice(bf16[9,9,8,385]{2,3,1,0:T(8,128)(2,1)} %pad.30), slice={[1:9:2], [1:9:2], [0:8:1], [2:385:2]} | slice | bytes 98304 | tf_op jit(solution)/shard_map/slice | solution.py:135
  273.5 9.6 %slice.190 = bf16[4,4,8,192]{2,3,1,0:T(8,128)(2,1)} slice(bf16[9,9,8,385]{2,3,1,0:T(8,128)(2,1)} %pad.30), slice={[1:9:2], [1:9:2], [0:8:1], [1:385:2]} | slice | bytes 98304 | tf_op jit(solution)/shard_map/slice | solution.py:135
  283.0 9.5 %slice.189 = bf16[4,4,8,192]{2,3,1,0:T(8,128)(2,1)} slice(bf16[9,9,8,385]{2,3,1,0:T(8,128)(2,1)} %pad.30), slice={[1:9:2], [1:9:2], [0:8:1], [0:384:2]} | slice | bytes 98304 | tf_op jit(solution)/shard_map/slice | solution.py:135
  292.6 9.6 %slice.188 = bf16[4,4,8,192]{2,3,1,0:T(8,128)(2,1)} slice(bf16[9,9,8,385]{2,3,1,0:T(8,128)(2,1)} %pad.30), slice={[1:9:2], [0:8:2], [0:8:1], [2:385:2]} | slice | bytes 98304 | tf_op jit(solution)/shard_map/slice | solution.py:135
  302.2 9.6 %slice.187 = bf16[4,4,8,192]{2,3,1,0:T(8,128)(2,1)} slice(bf16[9,9,8,385]{2,3,1,0:T(8,128)(2,1)} %pad.30), slice={[1:9:2], [0:8:2], [0:8:1], [1:385:2]} | slice | bytes 98304 | tf_op jit(solution)/shard_map/slice | solution.py:135
  311.7 9.6 %slice.186 = bf16[4,4,8,192]{2,3,1,0:T(8,128)(2,1)} slice(bf16[9,9,8,385]{2,3,1,0:T(8,128)(2,1)} %pad.30), slice={[1:9:2], [0:8:2], [0:8:1], [0:384:2]} | slice | bytes 98304 | tf_op jit(solution)/shard_map/slice | solution.py:135
  321.3 9.5 %slice.185 = bf16[4,4,8,192]{2,3,1,0:T(8,128)(2,1)} slice(bf16[9,9,8,385]{2,3,1,0:T(8,128)(2,1)} %pad.30), slice={[0:8:2], [2:9:2], [0:8:1], [2:385:2]} | slice | bytes 98304 | tf_op jit(solution)/shard_map/slice | solution.py:135
  330.8 9.5 %slice.184 = bf16[4,4,8,192]{2,3,1,0:T(8,128)(2,1)} slice(bf16[9,9,8,385]{2,3,1,0:T(8,128)(2,1)} %pad.30), slice={[0:8:2], [2:9:2], [0:8:1], [1:385:2]} | slice | bytes 98304 | tf_op jit(solution)/shard_map/slice | solution.py:135
  340.3 9.5 %slice.183 = bf16[4,4,8,192]{2,3,1,0:T(8,128)(2,1)} slice(bf16[9,9,8,385]{2,3,1,0:T(8,128)(2,1)} %pad.30), slice={[0:8:2], [2:9:2], [0:8:1], [0:384:2]} | slice | bytes 98304 | tf_op jit(solution)/shard_map/slice | solution.py:135
  349.7 9.6 %slice.182 = bf16[4,4,8,192]{2,3,1,0:T(8,128)(2,1)} slice(bf16[9,9,8,385]{2,3,1,0:T(8,128)(2,1)} %pad.30), slice={[0:8:2], [1:9:2], [0:8:1], [2:385:2]} | slice | bytes 98304 | tf_op jit(solution)/shard_map/slice | solution.py:135
  359.3 9.6 %slice.181 = bf16[4,4,8,192]{2,3,1,0:T(8,128)(2,1)} slice(bf16[9,9,8,385]{2,3,1,0:T(8,128)(2,1)} %pad.30), slice={[0:8:2], [1:9:2], [0:8:1], [1:385:2]} | slice | bytes 98304 | tf_op jit(solution)/shard_map/slice | solution.py:135
  368.9 9.6 %slice.180 = bf16[4,4,8,192]{2,3,1,0:T(8,128)(2,1)} slice(bf16[9,9,8,385]{2,3,1,0:T(8,128)(2,1)} %pad.30), slice={[0:8:2], [1:9:2], [0:8:1], [0:384:2]} | slice | bytes 98304 | tf_op jit(solution)/shard_map/slice | solution.py:135
  378.5 9.6 %slice.179 = bf16[4,4,8,192]{2,3,1,0:T(8,128)(2,1)} slice(bf16[9,9,8,385]{2,3,1,0:T(8,128)(2,1)} %pad.30), slice={[0:8:2], [0:8:2], [0:8:1], [2:385:2]} | slice | bytes 98304 | tf_op jit(solution)/shard_map/slice | solution.py:135
  388.0 9.6 %slice.178 = bf16[4,4,8,192]{2,3,1,0:T(8,128)(2,1)} slice(bf16[9,9,8,385]{2,3,1,0:T(8,128)(2,1)} %pad.30), slice={[0:8:2], [0:8:2], [0:8:1], [1:385:2]} | slice | bytes 98304 | tf_op jit(solution)/shard_map/slice | solution.py:135
  397.6 9.6 %slice.177 = bf16[4,4,8,192]{2,3,1,0:T(8,128)(2,1)} slice(bf16[9,9,8,385]{2,3,1,0:T(8,128)(2,1)} %pad.30), slice={[0:8:2], [0:8:2], [0:8:1], [0:384:2]} | slice | bytes 98304 | tf_op jit(solution)/shard_map/slice | solution.py:135
  407.2 17.8 %concatenate.31 = bf16[4,4,216,192]{2,3,1,0:T(8,128)(2,1)S(1)} concatenate(bf16[4,4,8,192]{2,3,1,0:T(8,128)(2,1)} %slice.177, bf16[4,4,8,192]{2,3,1,0:T(8,128)(2,1)} %slice.178, bf16[4,4,8,192]{2,3,1,0:T(8,128)(2,1)} %slice.179, bf16[4,4,8,192]{2,3,1,0:T(8,128)(2,1)} %slice.180, bf16[4,4,8,192]{2,3,1,0:T(8,128)(2,1)} %slice.181, bf16[4,4,8,192]{2,3,1,0:T(8,128)(2,1)} %slice.182, ...), dimensions={2} | concatenate | bytes 2654208 | tf_op jit(solution)/shard_map/concatenate | solution.py:142
  425.1 1.2 fusion.21
  (44 shorter events, 1.3 us)
Async XLA Ops:
  0.0 11.5 %copy-start = (bf16[32,2,32,384]{3,2,1,0:T(8,128)(2,1)S(1)}, bf16[32,2,32,384]{3,2,1,0:T(8,128)(2,1)}, u32[]{:S(2)}) copy-start(bf16[32,2,32,384]{3,2,1,0:T(8,128)(2,1)} %param.10) | copy-start | bytes 4718596
  11.5 7.9 %copy-start.7 = (s32[1,4,4]{2,1,0:T(4,128)S(1)}, s32[1,4,4]{2,1,0:T(4,128)}, u32[]{:S(2)}) copy-start(s32[1,4,4]{2,1,0:T(4,128)} %param.11) | copy-start | bytes 196
  11.6 8.7 %copy-start.4 = (bf16[8,32,384]{2,1,0:T(8,128)(2,1)S(1)}, bf16[8,32,384]{2,1,0:T(8,128)(2,1)}, u32[]{:S(2)}) copy-start(bf16[8,32,384]{2,1,0:T(8,128)(2,1)} %param.9) | copy-start | bytes 589828
  11.6 9.5 %copy-start.8 = (s32[8,4]{0,1:T(4,128)S(1)}, s32[8,4]{0,1:T(4,128)}, u32[]{:S(2)}) copy-start(s32[8,4]{0,1:T(4,128)} %param.13) | copy-start | bytes 388
  13.5 42.3 %all-to-all-start.1 = ((bf16[16,2,2,32,384]{4,3,2,1,0:T(8,128)(2,1)}), bf16[16,2,2,32,384]{4,3,2,1,0:T(8,128)(2,1)S(1)}, u32[]{:S(2)}, u32[]{:S(2)}) async-start(bf16[16,2,2,32,384]{4,3,2,1,0:T(8,128)(2,1)} %bitcast.2), calls=%async_computation.1 | async-start | bytes 3145728 | tf_op jit(solution)/shard_map/all_to_all | solution.py:104
  101.8 6.9 %copy-start.2 = (bf16[8,8,32,384]{3,2,1,0:T(8,128)(2,1)S(1)}, bf16[8,8,32,384]{3,2,1,0:T(8,128)(2,1)}, u32[]{:S(2)}) copy-start(bf16[8,8,32,384]{3,2,1,0:T(8,128)(2,1)} %copy.72) | copy-start | bytes 4718596
  101.8 6.9 %copy-start.3 = (f32[8,32,384]{2,1,0:T(8,128)S(1)}, f32[8,32,384]{2,1,0:T(8,128)}, u32[]{:S(2)}) copy-start(f32[8,32,384]{2,1,0:T(8,128)} %convert_element_type.61) | copy-start | bytes 1179652
  108.8 11.0 %copy-start.6 = (bf16[3,3,8,3,32]{4,2,3,1,0:T(8,128)(2,1)S(1)}, bf16[3,3,8,3,32]{4,2,3,1,0:T(8,128)(2,1)}, u32[]{:S(2)}) copy-start(bf16[3,3,8,3,32]{4,2,3,1,0:T(8,128)(2,1)} %param.14) | copy-start | bytes 41476
  113.1 8.0 %collective-permute-start = (bf16[8,1,32,384]{3,2,1,0:T(8,128)(2,1)S(1)}, bf16[8,1,32,384]{3,2,1,0:T(8,128)(2,1)S(1)}, u32[]{:S(2)}, u32[]{:S(2)}) collective-permute-start(bf16[8,1,32,384]{3,2,1,0:T(8,128)(2,1)S(1)} %get-tuple-element.8), channel_id=1, source_target_pairs={{0,1},{1,2},{2,3},{3,4},{4,5},{5,6},{6,7},{7,8},{8,9},{9,10},{10,1... | collective-permute-start | bytes 589832 | tf_op jit(solution)/shard_map/ppermute | solution.py:22
  115.0 7.7 %collective-permute-start.1 = (bf16[8,1,32,384]{3,2,1,0:T(8,128)(2,1)S(1)}, bf16[8,1,32,384]{3,2,1,0:T(8,128)(2,1)S(1)}, u32[]{:S(2)}, u32[]{:S(2)}) collective-permute-start(bf16[8,1,32,384]{3,2,1,0:T(8,128)(2,1)S(1)} %get-tuple-element.9), channel_id=1, source_target_pairs={{1,0},{2,1},{3,2},{4,3},{5,4},{6,5},{7,6},{8,7},{9,8},{10,9},{11,1... | collective-permute-start | bytes 589832 | tf_op jit(solution)/shard_map/ppermute | solution.py:23
  126.5 2.4 copy-start.10
  129.3 6.5 %collective-permute-start.2 = (bf16[8,1,8,384]{3,2,1,0:T(8,128)(2,1)S(1)}, bf16[8,1,8,384]{3,2,1,0:T(8,128)(2,1)S(1)}, u32[]{:S(2)}, u32[]{:S(2)}) collective-permute-start(bf16[8,1,8,384]{3,2,1,0:T(8,128)(2,1)S(1)} %slice.238), channel_id=1, source_target_pairs={{0,1},{1,2},{2,3},{3,4},{4,5},{5,6},{6,7},{7,8},{8,9},{9,10},{10,1... | collective-permute-start | bytes 147464 | tf_op jit(solution)/shard_map/ppermute | solution.py:31
  407.2 17.9 %copy-start.5 = (bf16[16,3,3,3,8]{0,4,3,2,1:T(8,128)(2,1)S(1)}, bf16[16,3,3,3,8]{0,4,3,2,1:T(8,128)(2,1)}, u32[]{:S(2)}) copy-start(bf16[16,3,3,3,8]{0,4,3,2,1:T(8,128)(2,1)} %param.16) | copy-start | bytes 20740
  407.2 17.9 %copy-start.9 = (f32[16]{0:T(128)S(1)}, f32[16]{0:T(128)}, u32[]{:S(2)}) copy-start(f32[16]{0:T(128)} %param.17) | copy-start | bytes 196
  407.2 19.1 %copy-start.1 = (bf16[32,2,32,384]{3,2,1,0:T(8,128)(2,1)S(1)}, bf16[32,2,32,384]{3,2,1,0:T(8,128)(2,1)}, u32[]{:S(2)}) copy-start(bf16[32,2,32,384]{3,2,1,0:T(8,128)(2,1)} %param.10) | copy-start | bytes 4718596
where the time goes:
time: 435 us; the launch traced here: 426 us
  local copies, waits for them, and re-layouts  347 us (80%)
  waiting for transfers between devices  41.1 us (9%)
  starting transfers between devices  14.7 us (3%)
  blocking collectives  10.1 us (2%)
  other arithmetic  8.42 us (2%)
    slice x27, local copies, waits for them, and re-layouts, on_device(): padded[plane_tap:plane_tap + 2 * half_p:2, row_tap:row_tap + 2 * half_r:2...  258 us
    gather x8, local copies, waits for them, and re-layouts, shifted(): return lax.dynamic_slice_in_dim(padded, SHIFT - offset, rows.shape[2], 2)  44.5 us
    all_to_all x1, waiting for transfers between devices, on_device(): lax.all_to_all(outgoing, 'view', split_axis=0, concat_axis=0, tiled=True)  33.9 us
    concatenate x1, local copies, waits for them, and re-layouts, on_device(): gathered = jnp.concatenate(tap_list, axis=2)  17.8 us
    all_to_all x1, blocking collectives, on_device(): lax.all_to_all(wanted, 'view', split_axis=0, concat_axis=0, tiled=True)  10.1 us
    pad x1, local copies, waits for them, and re-layouts, on_device(): padded = jnp.pad(stacked, ((1, 0), (0, 0), (0, 0), (1, 0)))  8.95 us
  transfers between devices with their start and end apart: 4, of which 4 were waited for; matrix products, arithmetic and copies ran while one was open for 0% of the time, Pallas kernels for 0%

commit v1 on v0

v1 whole, which is shorter than its diff:
```python
import jax
import jax.numpy as jnp
from jax import lax
from jax.experimental import pallas as pl
from jax.experimental.pallas import tpu as pltpu
from jax.sharding import PartitionSpec as P


def passed_along(x, axis, by):
    count = lax.axis_size(axis)
    pairs = [(i, i + by) for i in range(count) if 0 <= i + by < count]
    return lax.ppermute(x, axis, pairs)


def request_slots(flat_ids, slot_cap, tiles_dev):
    is_live = flat_ids >= 0
    owners = jnp.where(is_live, flat_ids // tiles_dev, -1)
    count_req = flat_ids.shape[0]
    earlier = jnp.arange(count_req)[None, :] < jnp.arange(count_req)[:, None]
    same_owner = (owners[:, None] == owners[None, :]) & earlier & is_live[None, :]
    slot_rank = jnp.sum(same_owner.astype(jnp.int32), axis=1)
    slot_ids = jnp.where(is_live, owners * slot_cap + slot_rank, -1)
    return (slot_ids, flat_ids % tiles_dev)


def request_table(slot_ids, local_ids, n_view, slot_cap):
    positions = jnp.arange(n_view * slot_cap)
    matches = slot_ids[:, None] == positions[None, :]
    wanted = jnp.sum(jnp.where(matches, local_ids[:, None] + 1, 0), axis=0) - 1
    return wanted.reshape(n_view, slot_cap)


def variance_kernel(slot_ref, disp_ref, count_ref, arrived_ref, ref_ref, out_ref, wide_ref):
    sources, blocks = slot_ref.shape
    planes = disp_ref.shape[0]
    tile_rows, n_cols = arrived_ref.shape[1:]
    live = count_ref[0]
    for source in range(sources):
        for block in range(blocks):
            slot = jnp.maximum(slot_ref[source, block], 0)
            tile = arrived_ref[slot].astype(jnp.float32)
            wide_ref[source, block * tile_rows : (block + 1) * tile_rows] = jnp.where(
                source < live, tile, 0.0
            )
    total = live.astype(jnp.float32) + 1.0
    inverse = 1.0 / jnp.full((1, n_cols), total, jnp.float32)
    chunk = 32
    column = lax.broadcasted_iota(jnp.int32, (chunk, n_cols), 1)

    def one_plane(plane, carry):
        offsets = [disp_ref[plane, source] for source in range(sources)]
        for row in range(ref_ref.shape[0] // chunk):
            at = slice(row * chunk, (row + 1) * chunk)
            summed = ref_ref[at].astype(jnp.float32)
            squares = summed * summed
            for source in range(sources):
                offset = offsets[source]
                turned = pltpu.roll(
                    wide_ref[source, at], jnp.where(offset < 0, offset + n_cols, offset), 1
                )
                origin = column - offset
                inside = (origin >= 0) & (origin < n_cols)
                turned = jnp.where(inside, turned, 0.0)
                summed = summed + turned
                squares = squares + turned * turned
            mean = summed * inverse
            out_ref[plane, at] = (squares * inverse - mean * mean).astype(jnp.bfloat16)
        return carry

    lax.fori_loop(0, planes, one_plane, 0)


def conv_kernel(
    first_strip_ref, var_ref, above_ref, below_ref, w1_ref, b1_ref, w2_ref, b2_ref, pick_ref,
    out_ref, acc_ref, cost_ref,
):
    planes, _, n_cols = var_ref.shape
    part = w1_ref.shape[0] // 9
    half_p, half_r, c2, half_x = out_ref.shape
    wide = pick_ref.shape[1] // 3
    weights = w1_ref[...]

    def one_plane(plane):
        block = jnp.concatenate([above_ref[plane], var_ref[plane], below_ref[plane]], axis=0)
        product = jnp.dot(weights, block, preferred_element_type=jnp.float32)
        for tap in range(3):
            target = plane + 1 - tap
            if 0 <= target < planes:
                piece = product[tap * 3 * part : (tap + 1) * 3 * part]
                if tap == 0 or (tap == 1 and plane == 0):
                    acc_ref[target] = piece
                else:
                    acc_ref[target] += piece

    column = lax.broadcasted_iota(jnp.int32, (part, n_cols), 1)
    row = lax.broadcasted_iota(jnp.int32, (part, n_cols), 0)
    hidden = (row < part // (var_ref.shape[1] // 32 + 2)) & (first_strip_ref[0] == 1)
    cost_ref[0] = jnp.zeros(cost_ref.shape[1:], cost_ref.dtype)

    def finish(plane):
        left = jnp.where(column == 0, 0.0, pltpu.roll(acc_ref[plane, 0:part], 1, 1))
        right = jnp.where(
            column == n_cols - 1, 0.0, pltpu.roll(acc_ref[plane, 2 * part : 3 * part], n_cols - 1, 1)
        )
        total = acc_ref[plane, part : 2 * part] + left + right + b1_ref[...]
        cost = jnp.where(hidden, 0.0, jnp.maximum(total, 0.0)).astype(jnp.bfloat16)
        spread = jnp.dot(cost, pick_ref[...], preferred_element_type=jnp.float32)
        spread = spread.astype(jnp.bfloat16)
        for tap in range(3):
            cost_ref[plane + 1, tap * part : (tap + 1) * part] = spread[
                :, tap * wide : (tap + 1) * wide
            ]

    def second(q):
        block = cost_ref[2 * q : 2 * q + 3].reshape(9 * part, wide)
        result = jnp.dot(w2_ref[...], block, preferred_element_type=jnp.float32)
        result = result + b2_ref[...]
        out_ref[q] = result[:, :half_x].reshape(half_r, c2, half_x)

    for plane in range(planes):
        one_plane(plane)
        if plane >= 1:
            finish(plane - 1)
            if plane % 2 == 0:
                second(plane // 2 - 1)
    finish(planes - 1)
    second(half_p - 1)


def banded_first(conv_first, rows_n):
    taps_p, taps_r, c1, taps_x, channels = conv_first.shape
    moved = jnp.transpose(conv_first, (0, 3, 2, 1, 4))
    bands = [
        jnp.pad(moved, ((0, 0), (0, 0), (0, 0), (hi, rows_n - hi), (0, 0))).reshape(
            taps_p, taps_x, c1, (rows_n + 3) * channels
        )
        for hi in range(rows_n + 1)
    ]
    bands.append(jnp.zeros_like(bands[0]))
    return jnp.stack(bands, axis=2).reshape(-1, (rows_n + 3) * channels)


def banded_second(conv_second, rows_n):
    c2, taps_p, taps_r, taps_x, c1 = conv_second.shape
    moved = jnp.transpose(conv_second, (0, 1, 3, 2, 4))
    bands = [
        jnp.pad(
            moved, ((0, 0), (0, 0), (0, 0), (2 * g, rows_n + 2 - taps_r - 2 * g), (0, 0))
        ).reshape(c2, -1)
        for g in range(rows_n // 2)
    ]
    return jnp.concatenate(bands, axis=0)


def on_device(
    ref_features,
    source_tiles,
    pair_lists,
    view_counts,
    disparities,
    conv_first,
    bias_first,
    conv_second,
    bias_second,
):
    n_view = lax.axis_size("view")
    rows_n, channels, n_cols = ref_features.shape
    tiles_dev = source_tiles.shape[0]
    _, sources, blocks = pair_lists.shape
    planes = disparities.shape[0]
    c1 = conv_first.shape[2]
    c2 = conv_second.shape[0]
    request_total = sources * blocks
    slot_cap = max(2, (request_total + n_view - 1) // n_view)
    flat_ids = pair_lists.reshape(request_total)
    slot_ids, local_ids = request_slots(flat_ids, slot_cap, tiles_dev)
    wanted = request_table(slot_ids, local_ids, n_view, slot_cap)
    outgoing = source_tiles[
        jnp.maximum(lax.all_to_all(wanted, "view", split_axis=0, concat_axis=0, tiled=True), 0)
    ]
    arrived = lax.all_to_all(outgoing, "view", split_axis=0, concat_axis=0, tiled=True)
    arrived = arrived.reshape(n_view * slot_cap, 2 * channels, n_cols)
    smem = pl.BlockSpec(memory_space=pltpu.SMEM)
    vmem = pl.BlockSpec(memory_space=pltpu.VMEM)
    volume = pl.pallas_call(
        variance_kernel,
        out_shape=jax.ShapeDtypeStruct((planes, rows_n * channels, n_cols), jnp.bfloat16),
        in_specs=[smem, smem, smem, vmem, vmem],
        out_specs=vmem,
        scratch_shapes=[pltpu.VMEM((sources, rows_n * channels, n_cols), jnp.float32)],
        name="variance",
    )(
        slot_ids.reshape(sources, blocks),
        disparities,
        view_counts,
        arrived,
        ref_features.reshape(rows_n * channels, n_cols),
    )
    above = passed_along(volume[:, (rows_n - 2) * channels :], "view", 1)
    below = passed_along(volume[:, :channels], "view", -1)
    w1 = banded_first(conv_first, rows_n)
    w2 = banded_second(conv_second, rows_n)
    part = (rows_n + 2) * c1
    half_x = n_cols // 2
    wide = -(-half_x // 128) * 128
    b1 = jnp.broadcast_to(bias_first[None, :, None], (rows_n + 2, c1, 1)).reshape(part, 1)
    b2 = jnp.broadcast_to(bias_second[None, :, None], (rows_n // 2, c2, 1)).reshape(-1, 1)
    x_in = jnp.arange(n_cols)[:, None, None]
    x_out = 2 * jnp.arange(wide)[None, None, :] + jnp.arange(3)[None, :, None] - 1
    pick = ((x_in == x_out) & (jnp.arange(wide) < half_x)).astype(jnp.bfloat16)
    pick = pick.reshape(n_cols, 3 * wide)
    first_strip = (lax.axis_index("view") == 0).astype(jnp.int32).reshape(1)
    return pl.pallas_call(
        conv_kernel,
        out_shape=jax.ShapeDtypeStruct((planes // 2, rows_n // 2, c2, half_x), jnp.float32),
        in_specs=[smem] + [vmem] * 8,
        out_specs=vmem,
        scratch_shapes=[
            pltpu.VMEM((planes, 3 * part, n_cols), jnp.float32),
            pltpu.VMEM((planes + 1, 3 * part, wide), jnp.bfloat16),
        ],
        name="convolutions",
    )(first_strip, volume, above, below, w1, b1, w2, b2, pick)


def solution(mesh):
    return jax.shard_map(
        on_device,
        mesh=mesh,
        in_specs=(
            P(("groups", "view"), None, None),
            P(("groups", "view"), None, None, None),
            P(("groups", "view"), None, None),
            P(("groups", "view")),
            P("groups", None),
            P(),
            P(),
            P(),
            P(),
        ),
        out_specs=P("groups", "view", None, None),
        check_vma=False,
    )
```

time: 435 us -> 93.1 us (0.21)
  the two profiles are of different devices: /device:TPU:16 before, /device:TPU:15 now
where the time goes in v1:
time: 93.1 us; the launch traced here: 91.9 us
  local copies, waits for them, and re-layouts  36.9 us (40%)
  Pallas kernels  15.8 us (17%)
  waiting for transfers between devices  13 us (14%)
  starting transfers between devices  11.8 us (13%)
  blocking collectives  10.2 us (11%)
  other arithmetic  3.35 us (4%)
    another operation x11, local copies, waits for them, and re-layouts, banded_first(): return jnp.stack(bands, axis=2).reshape(-1, (rows_n + 3) * channels)  15.8 us
    all_to_all x1, blocking collectives, on_device(): lax.all_to_all(wanted, 'view', split_axis=0, concat_axis=0, tiled=True)  10.2 us
    unnamed x31, local copies, waits for them, and re-layouts  10 us
    pallas_call x1, Pallas kernels, on_device(): pl.pallas_call(conv_kernel, out_shape=jax.ShapeDtypeStruct((planes // 2,...  8.7 us
    all_to_all x1, waiting for transfers between devices, on_device(): lax.all_to_all(outgoing, 'view', split_axis=0, concat_axis=0, tiled=True)  8.09 us
    pallas_call x1, Pallas kernels, on_device(): pl.pallas_call(variance_kernel, out_shape=jax.ShapeDtypeStruct((planes, r...  7.08 us
    all_to_all x1, starting transfers between devices, on_device(): lax.all_to_all(outgoing, 'view', split_axis=0, concat_axis=0, tiled=True)  6.34 us
    ppermute x2, starting transfers between devices, passed_along(): return lax.ppermute(x, axis, pairs)  5.47 us
  transfers between devices with their start and end apart: 3, of which 2 were waited for; matrix products, arithmetic and copies ran while one was open for 36% of the time, Pallas kernels for 0%

profile of v1, /device:TPU:15, one launch (start us, length us, event | category | flops | bytes accessed | tf_op | source)
XLA Modules:
  0.0 91.9 jit_solution(17624089705230186069)
XLA Ops:
  0.0 0.0 copy-start
  0.0 0.9 reshape.226
  0.9 0.2 convert_reduce_fusion
  1.1 0.1 select_reduce_fusion
  1.2 0.1 sub.21
  1.3 10.2 %all_to_all.11 = s32[16,1,2]{2,1,0:T(1,128)S(1)} all-to-all(s32[16,1,2]{2,1,0:T(1,128)S(1)} %bitcast.43), channel_id=1, replica_groups=mesh['groups'=2,'view'=16] {'view'}, dimensions={0} | all-to-all | bytes 256 | tf_op jit(solution)/shard_map/all_to_all | solution.py:179
  11.5 0.1 reshape.238
  11.6 0.0 copy-done
  11.6 1.9 %gather_fusion = bf16[32,2,32,384]{3,2,1,0:T(8,128)(2,1)} fusion(bf16[32,2,32,384]{3,2,1,0:T(8,128)(2,1)S(1)} %copy-done, s32[1024]{0:T(1024)S(1)} %pad_clamp_fusion), kind=kCustom, calls=%fused_computation | custom fusion | bytes 3145856 | tf_op jit(solution)/shard_map/gather | solution.py:178
  13.5 0.0 copy-start.7
  13.5 6.3 %all-to-all-start.1 = ((bf16[16,2,2,32,384]{4,3,2,1,0:T(8,128)(2,1)}), bf16[16,2,2,32,384]{4,3,2,1,0:T(8,128)(2,1)S(1)}, u32[]{:S(2)}, u32[]{:S(2)}) async-start(bf16[16,2,2,32,384]{4,3,2,1,0:T(8,128)(2,1)} %bitcast.35), calls=%async_computation.1 | async-start | bytes 3145728 | tf_op jit(solution)/shard_map/all_to_all | solution.py:181
  19.9 0.7 reduce_sum.21
  20.5 0.0 copy-done.7
  20.6 1.8 %fusion.13 = (bf16[3,3,8,11,32]{4,3,2,1,0:T(8,128)(2,1)S(1)}, bf16[3,3,8,11,32]{4,3,2,1,0:T(8,128)(2,1)}, bf16[3,3,8,11,32]{4,3,2,1,0:T(8,128)(2,1)}, bf16[3,3,8...) fusion(bf16[3,3,8,3,32]{4,3,2,1,0:T(4,128)(2,1)S(1)} %copy.82), kind=kLoop, calls=%fused_computation.50 | loop fusion | bytes 470016 | tf_op jit(solution)/shard_map/jit(_pad)/pad | solution.py:134
  22.4 1.8 %stack_reshape.27 = bf16[3,3,1,8,352]{4,3,1,0,2:T(8,128)(2,1)} reshape(bf16[3,3,8,11,32]{4,3,2,1,0:T(8,128)(2,1)} %get-tuple-element.13) | data formatting | bytes 101376 | tf_op jit(solution)/shard_map/stack;reshape | solution.py:140
  24.2 1.8 %stack_reshape.28 = bf16[3,3,1,8,352]{4,3,1,0,2:T(8,128)(2,1)} reshape(bf16[3,3,8,11,32]{4,3,2,1,0:T(8,128)(2,1)} %get-tuple-element.12) | data formatting | bytes 101376 | tf_op jit(solution)/shard_map/stack;reshape | solution.py:140
  26.0 1.8 %stack_reshape.29 = bf16[3,3,1,8,352]{4,3,1,0,2:T(8,128)(2,1)} reshape(bf16[3,3,8,11,32]{4,3,2,1,0:T(8,128)(2,1)} %get-tuple-element.11) | data formatting | bytes 101376 | tf_op jit(solution)/shard_map/stack;reshape | solution.py:140
  27.8 1.8 %stack_reshape.30 = bf16[3,3,1,8,352]{4,3,1,0,2:T(8,128)(2,1)} reshape(bf16[3,3,8,11,32]{4,3,2,1,0:T(8,128)(2,1)} %get-tuple-element.10) | data formatting | bytes 101376 | tf_op jit(solution)/shard_map/stack;reshape | solution.py:140
  29.5 1.8 %stack_reshape.31 = bf16[3,3,1,8,352]{4,3,1,0,2:T(8,128)(2,1)} reshape(bf16[3,3,8,11,32]{4,3,2,1,0:T(8,128)(2,1)} %get-tuple-element.9) | data formatting | bytes 101376 | tf_op jit(solution)/shard_map/stack;reshape | solution.py:140
  31.3 1.8 %stack_reshape.32 = bf16[3,3,1,8,352]{4,3,1,0,2:T(8,128)(2,1)} reshape(bf16[3,3,8,11,32]{4,3,2,1,0:T(8,128)(2,1)} %get-tuple-element.8) | data formatting | bytes 101376 | tf_op jit(solution)/shard_map/stack;reshape | solution.py:140
  33.1 1.8 %stack_reshape.33 = bf16[3,3,1,8,352]{4,3,1,0,2:T(8,128)(2,1)} reshape(bf16[3,3,8,11,32]{4,3,2,1,0:T(8,128)(2,1)} %get-tuple-element.7) | data formatting | bytes 101376 | tf_op jit(solution)/shard_map/stack;reshape | solution.py:140
  34.9 1.2 %stack_reshape.34 = bf16[3,3,1,8,352]{4,3,1,0,2:T(8,128)(2,1)S(1)} reshape(bf16[3,3,8,11,32]{4,3,2,1,0:T(8,128)(2,1)} %get-tuple-element.6) | data formatting | bytes 101376 | tf_op jit(solution)/shard_map/stack;reshape | solution.py:140
  36.1 0.2 stack_reshape.35
  36.3 1.4 %copy.61.disp_ref = s32[8,4]{1,0:T(8,128)} copy(s32[8,4]{0,1:T(4,128)} %param.13) | data formatting | bytes 256 | tf_op args[4]
  38.3 0.8 constant_dynamic-update-slice_fusion.8
  39.1 0.8 constant_dynamic-update-slice_fusion.7
  39.9 0.8 constant_dynamic-update-slice_fusion.6
  40.7 0.8 constant_dynamic-update-slice_fusion.5
  41.6 0.8 constant_dynamic-update-slice_fusion.4
  42.4 0.8 constant_dynamic-update-slice_fusion.3
  43.2 0.8 constant_dynamic-update-slice_fusion.2
  44.1 0.0 copy-start.4
  44.1 0.8 copy-done.4
  44.9 1.3 %fusion.8.slot_ref = s32[4,4]{1,0:T(4,128)} fusion(s32[4,4]{1,0:T(4,128)} %reduce_sum.21, s32[1,4,4]{2,1,0:T(4,128)} %param.11), kind=kLoop, calls=%fused_computation.32 | loop fusion | flops 320 | bytes 192 | tf_op jit(solution)/shard_map/jit(_where)/select_n | solution.py:22
  46.2 1.8 %fusion.14 = (bf16[16,3,3,10,8]{0,4,3,2,1:T(8,128)(2,1)}, bf16[16,3,3,10,8]{0,4,3,2,1:T(8,128)(2,1)S(1)}, bf16[16,3,3,10,8]{0,4,3,2,1:T(8,128)(2,1)S(1)}, bf16[16,3,3,10,8]{0,4,3,2,1:T(8,128)(2,1)}) fusion(bf16[16,3,3,3,8]{0,4,3,2,1:T(8,128)(2,1)} %param.16), kind=kLoop, calls=%fused_computation.51 | loop fusion | bytes 99072 | tf_op jit(solution)/shard_map/jit(_pad)/pad | solution.py:147
  48.0 8.1 %all-to-all-done.1 = bf16[16,2,2,32,384]{4,3,2,1,0:T(8,128)(2,1)S(1)} async-done(((bf16[16,2,2,32,384]{4,3,2,1,0:T(8,128)(2,1)}), bf16[16,2,2,32,384]{4,3,2,1,0:T(8,128)(2,1)S(1)}, u32[]{:S(2)}, u32[]{:S(2)}) %all-to-all-start.1) | async-done | bytes 1572896 | tf_op jit(solution)/shard_map/all_to_all | solution.py:181
  56.1 0.0 copy-start.1
  56.1 1.1 %copy-done.1 = bf16[16,2,2,32,384]{4,3,2,1,0:T(8,128)(2,1)} copy-done((bf16[16,2,2,32,384]{4,3,2,1,0:T(8,128)(2,1)}, bf16[16,2,2,32,384]{4,3,2,1,0:T(8,128)(2,1)S(1)}, u32[]{:S(2)}) %copy-start.1) | copy-done | bytes 1572888
  57.2 7.1 %variance.1.var_ref = bf16[8,256,384]{2,1,0:T(8,128)(2,1)} custom-call(s32[4,4]{1,0:T(4,128)} %fusion.8.slot_ref, s32[8,4]{1,0:T(8,128)} %copy.61.disp_ref, s32[1]{0:T(128)S(6)} %copy.106.count_ref, bf16[32,64,384]{2,1,0:T(8,128)(2,1)} %bitcast.34, bf16[256,384]{1,0:T(8,128)(2,1)} %bitcast.41), custom_call_target="tpu_custom_call" | custom-call | tf_op jit(solution)/shard_map/variance/pallas_call | solution.py:185
  64.3 0.0 copy-start.3
  64.3 0.0 copy-start.2
  64.3 0.0 copy-start.9
  64.3 1.1 %slice.10 = bf16[8,64,384]{2,1,0:T(8,128)(2,1)S(1)} slice(bf16[8,256,384]{2,1,0:T(8,128)(2,1)} %variance.1.var_ref), slice={[0:8], [192:256], [0:384]} | slice | bytes 786432 | tf_op jit(solution)/shard_map/slice | solution.py:199
  65.4 3.5 %collective-permute-start = (bf16[8,64,384]{2,1,0:T(8,128)(2,1)S(1)}, bf16[8,64,384]{2,1,0:T(8,128)(2,1)S(1)}, u32[]{:S(2)}, u32[]{:S(2)}) collective-permute-start(bf16[8,64,384]{2,1,0:T(8,128)(2,1)S(1)} %slice.10), channel_id=1, source_target_pairs={{0,1},{1,2},{2,3},{3,4},{4,5},{5,6},{6,7},{7,8},{8,9},{9,10},{10,1... | collective-permute-start | bytes 1179656 | tf_op jit(solution)/shard_map/ppermute | solution.py:12
  69.0 1.9 %copy.71 = bf16[3,3,10,8,352]{4,3,2,1,0:T(8,128)(2,1)} copy(bf16[3,3,10,8,352]{4,3,1,0,2:T(8,128)(2,1)} %copy-done.4) | data formatting | bytes 1013760 | tf_op jit(solution)/shard_map/stack | solution.py:140
  70.9 0.0 copy-done.3
  70.9 0.1 copy.76
  71.0 0.0 copy-done.2
  71.0 0.1 copy.77
  71.1 0.1 copy.78
  71.2 0.1 copy.79
  71.4 0.0 copy-done.8
  71.4 0.7 broadcast_in_dim.29.b1_ref
  72.1 0.0 copy-done.9
  72.1 0.7 broadcast_in_dim.30.b2_ref
  72.8 0.7 pad_maximum_fusion.w2_ref
  73.5 0.9 %slice.11 = bf16[8,32,384]{2,1,0:T(8,128)(2,1)S(1)} slice(bf16[8,256,384]{2,1,0:T(8,128)(2,1)} %variance.1.var_ref), slice={[0:8], [0:32], [0:384]} | slice | bytes 393216 | tf_op jit(solution)/shard_map/slice | solution.py:200
  74.4 1.9 %collective-permute-start.1 = (bf16[8,32,384]{2,1,0:T(8,128)(2,1)S(1)}, bf16[8,32,384]{2,1,0:T(8,128)(2,1)S(1)}, u32[]{:S(2)}, u32[]{:S(2)}) collective-permute-start(bf16[8,32,384]{2,1,0:T(8,128)(2,1)S(1)} %slice.11), channel_id=1, source_target_pairs={{1,0},{2,1},{3,2},{4,3},{5,4},{6,5},{7,6},{8,7},{9,8},{10,9},{11,1... | collective-permute-start | bytes 589832 | tf_op jit(solution)/shard_map/ppermute | solution.py:12
  76.4 1.0 %fusion.1.pick_ref = bf16[384,768]{1,0:T(8,128)(2,1)} fusion(s32[768]{0:T(1024)S(1)} %sub.23, pred[768]{0:T(1024)(128)(4,1)S(1)} %and.75), kind=kLoop, calls=%fused_computation.3 | loop fusion | flops 884736 | bytes 593664 | tf_op jit(solution)/shard_map/convert_element_type | solution.py:210
  77.4 4.9 %collective-permute-done.1.below_ref = bf16[8,32,384]{2,1,0:T(8,128)(2,1)S(1)} collective-permute-done((bf16[8,32,384]{2,1,0:T(8,128)(2,1)S(1)}, bf16[8,32,384]{2,1,0:T(8,128)(2,1)S(1)}, u32[]{:S(2)}, u32[]{:S(2)}) %collective-permute-start.1) | collective-permute-done | bytes 196640 | tf_op jit(solution)/shard_map/ppermute | solution.py:12
  82.3 0.0 collective-permute-done.above_ref
  82.3 0.7 copy-done.6
  83.0 0.2 copy-done.5
  83.2 8.7 %convolutions.1 = f32[4,4,16,192]{3,2,1,0:T(8,128)} custom-call(s32[1]{0:T(128)} %bitcast.first_strip_ref, bf16[8,256,384]{2,1,0:T(8,128)(2,1)} %variance.1.var_ref, bf16[8,64,384]{2,1,0:T(8,128)(2,1)} %copy-done.5, bf16[8,32,384]{2,1,0:T(8,128)(2,1)} %copy-done.6, bf16[720,352]{1,0:T(8,128)(2,1)} %bitcast.36, f32[80,1]{1,0:T(8,128)} %broadcast_in_dim.29.b1_ref, ...), custom_call_target="tpu_custom_call" | custom-call | tf_op jit(solution)/shard_map/convolutions/pallas_call | solution.py:213
  (21 shorter events, 0.2 us)
Async XLA Ops:
  0.0 11.6 %copy-start = (bf16[32,2,32,384]{3,2,1,0:T(8,128)(2,1)S(1)}, bf16[32,2,32,384]{3,2,1,0:T(8,128)(2,1)}, u32[]{:S(2)}) copy-start(bf16[32,2,32,384]{3,2,1,0:T(8,128)(2,1)} %param.10) | copy-start | bytes 4718596
  13.5 7.0 %copy-start.7 = (bf16[3,3,8,3,32]{4,2,3,1,0:T(8,128)(2,1)S(1)}, bf16[3,3,8,3,32]{4,2,3,1,0:T(8,128)(2,1)}, u32[]{:S(2)}) copy-start(bf16[3,3,8,3,32]{4,2,3,1,0:T(8,128)(2,1)} %param.14) | copy-start | bytes 41476
  13.5 42.5 %all-to-all-start.1 = ((bf16[16,2,2,32,384]{4,3,2,1,0:T(8,128)(2,1)}), bf16[16,2,2,32,384]{4,3,2,1,0:T(8,128)(2,1)S(1)}, u32[]{:S(2)}, u32[]{:S(2)}) async-start(bf16[16,2,2,32,384]{4,3,2,1,0:T(8,128)(2,1)} %bitcast.35), calls=%async_computation.1 | async-start | bytes 3145728 | tf_op jit(solution)/shard_map/all_to_all | solution.py:181
  44.1 0.8 copy-start.4
  56.1 1.2 %copy-start.1 = (bf16[16,2,2,32,384]{4,3,2,1,0:T(8,128)(2,1)}, bf16[16,2,2,32,384]{4,3,2,1,0:T(8,128)(2,1)S(1)}, u32[]{:S(2)}) copy-start(bf16[16,2,2,32,384]{4,3,2,1,0:T(8,128)(2,1)S(1)} %all-to-all-done.1) | copy-start | bytes 4718596
  64.3 6.6 %copy-start.3 = (bf16[16,3,3,10,8]{0,4,3,2,1:T(8,128)(2,1)S(1)}, bf16[16,3,3,10,8]{0,4,3,2,1:T(8,128)(2,1)}, u32[]{:S(2)}) copy-start(bf16[16,3,3,10,8]{0,4,3,2,1:T(8,128)(2,1)} %get-tuple-element.14) | copy-start | bytes 69124
  64.3 6.7 %copy-start.2 = (bf16[16,3,3,10,8]{0,4,3,2,1:T(8,128)(2,1)S(1)}, bf16[16,3,3,10,8]{0,4,3,2,1:T(8,128)(2,1)}, u32[]{:S(2)}) copy-start(bf16[16,3,3,10,8]{0,4,3,2,1:T(8,128)(2,1)} %get-tuple-element.17) | copy-start | bytes 69124
  64.3 7.1 %copy-start.8 = (f32[8]{0:T(128)S(1)}, f32[8]{0:T(128)}, u32[]{:S(2)}) copy-start(f32[8]{0:T(128)} %param.15) | copy-start | bytes 100
  64.3 7.8 %copy-start.9 = (f32[16]{0:T(128)S(1)}, f32[16]{0:T(128)}, u32[]{:S(2)}) copy-start(f32[16]{0:T(128)} %param.17) | copy-start | bytes 196
  65.4 16.9 %collective-permute-start = (bf16[8,64,384]{2,1,0:T(8,128)(2,1)S(1)}, bf16[8,64,384]{2,1,0:T(8,128)(2,1)S(1)}, u32[]{:S(2)}, u32[]{:S(2)}) collective-permute-start(bf16[8,64,384]{2,1,0:T(8,128)(2,1)S(1)} %slice.10), channel_id=1, source_target_pairs={{0,1},{1,2},{2,3},{3,4},{4,5},{5,6},{6,7},{7,8},{8,9},{9,10},{10,1... | collective-permute-start | bytes 1179656 | tf_op jit(solution)/shard_map/ppermute | solution.py:12
  74.4 7.9 %collective-permute-start.1 = (bf16[8,32,384]{2,1,0:T(8,128)(2,1)S(1)}, bf16[8,32,384]{2,1,0:T(8,128)(2,1)S(1)}, u32[]{:S(2)}, u32[]{:S(2)}) collective-permute-start(bf16[8,32,384]{2,1,0:T(8,128)(2,1)S(1)} %slice.11), channel_id=1, source_target_pairs={{1,0},{2,1},{3,2},{4,3},{5,4},{6,5},{7,6},{8,7},{9,8},{10,9},{11,1... | collective-permute-start | bytes 589832 | tf_op jit(solution)/shard_map/ppermute | solution.py:12
  82.3 0.7 copy-start.6
  82.3 0.8 copy-start.5

commit v2 on v1

--- a/solution.py
+++ b/solution.py
@@ -1,3 +1,5 @@
+import functools
+
 import jax
 import jax.numpy as jnp
 from jax import lax
@@ -30,58 +32,112 @@
     return wanted.reshape(n_view, slot_cap)
 
 
-def variance_kernel(slot_ref, disp_ref, count_ref, arrived_ref, ref_ref, out_ref, wide_ref):
-    sources, blocks = slot_ref.shape
+def variance_kernel(rows, slot_ref, disp_ref, count_ref, arrived_ref, ref_ref, *refs):
+    out_refs, wide_ref = refs[:-1], refs[-1]
+    sources = slot_ref.shape[0]
     planes = disp_ref.shape[0]
     tile_rows, n_cols = arrived_ref.shape[1:]
+    chunk = tile_rows // 2
     live = count_ref[0]
+    flat_rows = [row for group in rows for row in group]
     for source in range(sources):
-        for block in range(blocks):
-            slot = jnp.maximum(slot_ref[source, block], 0)
-            tile = arrived_ref[slot].astype(jnp.float32)
-            wide_ref[source, block * tile_rows : (block + 1) * tile_rows] = jnp.where(
-                source < live, tile, 0.0
-            )
+        for place, row in enumerate(flat_rows):
+            slot = jnp.maximum(slot_ref[source, row // 2], 0)
+            start = (row % 2) * chunk
+            tile = arrived_ref[slot, start : start + chunk].astype(jnp.float32)
+            wide_ref[source, place] = jnp.where(source < live, tile, 0.0)
     total = live.astype(jnp.float32) + 1.0
     inverse = 1.0 / jnp.full((1, n_cols), total, jnp.float32)
-    chunk = 32
     column = lax.broadcasted_iota(jnp.int32, (chunk, n_cols), 1)
 
     def one_plane(plane, carry):
         offsets = [disp_ref[plane, source] for source in range(sources)]
-        for row in range(ref_ref.shape[0] // chunk):
-            at = slice(row * chunk, (row + 1) * chunk)
-            summed = ref_ref[at].astype(jnp.float32)
-            squares = summed * summed
-            for source in range(sources):
-                offset = offsets[source]
-                turned = pltpu.roll(
-                    wide_ref[source, at], jnp.where(offset < 0, offset + n_cols, offset), 1
-                )
-                origin = column - offset
-                inside = (origin >= 0) & (origin < n_cols)
-                turned = jnp.where(inside, turned, 0.0)
-                summed = summed + turned
-                squares = squares + turned * turned
-            mean = summed * inverse
-            out_ref[plane, at] = (squares * inverse - mean * mean).astype(jnp.bfloat16)
+        place = 0
+        for group, out_ref in zip(rows, out_refs):
+            for at, row in enumerate(group):
+                summed = ref_ref[row * chunk : (row + 1) * chunk].astype(jnp.float32)
+                squares = summed * summed
+                for source in range(sources):
+                    offset = offsets[source]
+                    turned = pltpu.roll(
+                        wide_ref[source, place], jnp.where(offset < 0, offset + n_cols, offset), 1
+                    )
+                    origin = column - offset
+                    inside = (origin >= 0) & (origin < n_cols)
+                    turned = jnp.where(inside, turned, 0.0)
+                    summed = summed + turned
+                    squares = squares + turned * turned
+                mean = summed * inverse
+                out_ref[plane, at * chunk : (at + 1) * chunk] = (
+                    squares * inverse - mean * mean
+                ).astype(jnp.bfloat16)
+                place += 1
         return carry
 
     lax.fori_loop(0, planes, one_plane, 0)
 
 
+def variance(rows, slots, disparities, view_counts, arrived, ref_flat):
+    planes = disparities.shape[0]
+    sources = slots.shape[0]
+    chunk, n_cols = (arrived.shape[1] // 2, arrived.shape[2])
+    smem = pl.BlockSpec(memory_space=pltpu.SMEM)
+    vmem = pl.BlockSpec(memory_space=pltpu.VMEM)
+    count = sum(len(group) for group in rows)
+    values = planes * count * chunk * n_cols
+    return pl.pallas_call(
+        functools.partial(variance_kernel, rows),
+        out_shape=[
+            jax.ShapeDtypeStruct((planes, len(group) * chunk, n_cols), jnp.bfloat16)
+            for group in rows
+        ],
+        in_specs=[smem, smem, smem, vmem, vmem],
+        out_specs=[vmem] * len(rows),
+        scratch_shapes=[pltpu.VMEM((sources, count, chunk, n_cols), jnp.float32)],
+        cost_estimate=pl.CostEstimate(
+            flops=values * 40, bytes_accessed=values * 4, transcendentals=0
+        ),
+        compiler_params=pltpu.CompilerParams(vmem_limit_bytes=12 << 20),
+        name="variance%d" % count,
+    )(slots, disparities, view_counts, arrived, ref_flat)
+
+
+def prepare_kernel(conv_ref, w1_ref, pick_ref):
+    groups, c1, n_lanes = conv_ref.shape
+    rows_out = w1_ref.shape[0] // (groups * c1)
+    width = w1_ref.shape[1]
+    channels = width // (rows_out + 1)
+    for group in range(groups):
+        base = conv_ref[group].astype(jnp.float32)
+        pieces = [
+            pltpu.roll(base, hi * channels, 1) if hi else base for hi in range(rows_out - 1)
+        ]
+        pieces.append(jnp.zeros_like(base))
+        band = jnp.concatenate(pieces, axis=0).astype(jnp.bfloat16)
+        size = rows_out * c1
+        w1_ref[group * size : (group + 1) * size] = band[:, :width]
+    n_cols = pick_ref.shape[0]
+    wide = pick_ref.shape[1] // 3
+    source = lax.broadcasted_iota(jnp.int32, (n_cols, wide), 0)
+    target = lax.broadcasted_iota(jnp.int32, (n_cols, wide), 1)
+    for tap in range(3):
+        hit = (source == 2 * target + (tap - 1)) & (target < n_cols // 2)
+        pick_ref[:, tap * wide : (tap + 1) * wide] = jnp.where(hit, 1.0, 0.0).astype(jnp.bfloat16)
+
+
 def conv_kernel(
-    first_strip_ref, var_ref, above_ref, below_ref, w1_ref, b1_ref, w2_ref, b2_ref, pick_ref,
+    first_strip_ref, above_ref, top_ref, mid_ref, low_ref, below_ref, w1_ref, b1_ref, w2_ref, b2_ref, pick_ref,
     out_ref, acc_ref, cost_ref,
 ):
-    planes, _, n_cols = var_ref.shape
+    planes, _, n_cols = mid_ref.shape
     part = w1_ref.shape[0] // 9
     half_p, half_r, c2, half_x = out_ref.shape
     wide = pick_ref.shape[1] // 3
     weights = w1_ref[...]
 
     def one_plane(plane):
-        block = jnp.concatenate([above_ref[plane], var_ref[plane], below_ref[plane]], axis=0)
+        strips = (above_ref, top_ref, mid_ref, low_ref, below_ref)
+        block = jnp.concatenate([strip[plane] for strip in strips], axis=0)
         product = jnp.dot(weights, block, preferred_element_type=jnp.float32)
         for tap in range(3):
             target = plane + 1 - tap
@@ -94,7 +150,7 @@
 
     column = lax.broadcasted_iota(jnp.int32, (part, n_cols), 1)
     row = lax.broadcasted_iota(jnp.int32, (part, n_cols), 0)
-    hidden = (row < part // (var_ref.shape[1] // 32 + 2)) & (first_strip_ref[0] == 1)
+    hidden = (row < part // (2 * half_r + 2)) & (first_strip_ref[0] == 1)
     cost_ref[0] = jnp.zeros(cost_ref.shape[1:], cost_ref.dtype)
 
     def finish(plane):
@@ -127,17 +183,26 @@
     second(half_p - 1)
 
 
-def banded_first(conv_first, rows_n):
+def prepare(conv_first, rows_n, n_cols, wide):
     taps_p, taps_r, c1, taps_x, channels = conv_first.shape
-    moved = jnp.transpose(conv_first, (0, 3, 2, 1, 4))
-    bands = [
-        jnp.pad(moved, ((0, 0), (0, 0), (0, 0), (hi, rows_n - hi), (0, 0))).reshape(
-            taps_p, taps_x, c1, (rows_n + 3) * channels
-        )
-        for hi in range(rows_n + 1)
-    ]
-    bands.append(jnp.zeros_like(bands[0]))
-    return jnp.stack(bands, axis=2).reshape(-1, (rows_n + 3) * channels)
+    width = (rows_n + 3) * channels
+    lanes = -(-width // 128) * 128
+    groups = taps_p * taps_x
+    moved = jnp.transpose(conv_first, (0, 3, 2, 1, 4)).reshape(groups, c1, taps_r * channels)
+    moved = jnp.pad(moved, ((0, 0), (0, 0), (0, lanes - taps_r * channels)))
+    vmem = pl.BlockSpec(memory_space=pltpu.VMEM)
+    return pl.pallas_call(
+        prepare_kernel,
+        out_shape=[
+            jax.ShapeDtypeStruct((groups * (rows_n + 2) * c1, width), jnp.bfloat16),
+            jax.ShapeDtypeStruct((n_cols, 3 * wide), jnp.bfloat16),
+        ],
+        in_specs=[vmem],
+        out_specs=[vmem] * 2,
+        cost_estimate=pl.CostEstimate(flops=2000000, bytes_accessed=1200000, transcendentals=0),
+        compiler_params=pltpu.CompilerParams(vmem_limit_bytes=8 << 20),
+        name="prepare",
+    )(moved)
 
 
 def banded_second(conv_second, rows_n):
@@ -175,52 +240,42 @@
     flat_ids = pair_lists.reshape(request_total)
     slot_ids, local_ids = request_slots(flat_ids, slot_cap, tiles_dev)
     wanted = request_table(slot_ids, local_ids, n_view, slot_cap)
-    outgoing = source_tiles[
-        jnp.maximum(lax.all_to_all(wanted, "view", split_axis=0, concat_axis=0, tiled=True), 0)
-    ]
+    asked = lax.all_to_all(wanted, "view", split_axis=0, concat_axis=0, tiled=True)
+    outgoing = source_tiles[jnp.maximum(asked, 0)]
     arrived = lax.all_to_all(outgoing, "view", split_axis=0, concat_axis=0, tiled=True)
     arrived = arrived.reshape(n_view * slot_cap, 2 * channels, n_cols)
-    smem = pl.BlockSpec(memory_space=pltpu.SMEM)
-    vmem = pl.BlockSpec(memory_space=pltpu.VMEM)
-    volume = pl.pallas_call(
-        variance_kernel,
-        out_shape=jax.ShapeDtypeStruct((planes, rows_n * channels, n_cols), jnp.bfloat16),
-        in_specs=[smem, smem, smem, vmem, vmem],
-        out_specs=vmem,
-        scratch_shapes=[pltpu.VMEM((sources, rows_n * channels, n_cols), jnp.float32)],
-        name="variance",
-    )(
-        slot_ids.reshape(sources, blocks),
-        disparities,
-        view_counts,
-        arrived,
-        ref_features.reshape(rows_n * channels, n_cols),
-    )
-    above = passed_along(volume[:, (rows_n - 2) * channels :], "view", 1)
-    below = passed_along(volume[:, :channels], "view", -1)
-    w1 = banded_first(conv_first, rows_n)
     w2 = banded_second(conv_second, rows_n)
     part = (rows_n + 2) * c1
     half_x = n_cols // 2
     wide = -(-half_x // 128) * 128
     b1 = jnp.broadcast_to(bias_first[None, :, None], (rows_n + 2, c1, 1)).reshape(part, 1)
     b2 = jnp.broadcast_to(bias_second[None, :, None], (rows_n // 2, c2, 1)).reshape(-1, 1)
-    x_in = jnp.arange(n_cols)[:, None, None]
-    x_out = 2 * jnp.arange(wide)[None, None, :] + jnp.arange(3)[None, :, None] - 1
-    pick = ((x_in == x_out) & (jnp.arange(wide) < half_x)).astype(jnp.bfloat16)
-    pick = pick.reshape(n_cols, 3 * wide)
+    w1, pick = prepare(conv_first, rows_n, n_cols, wide)
+    ready = (arrived, w1, w2, b1, b2, pick)
+    arrived, w1, w2, b1, b2, pick = lax.optimization_barrier(ready)
+    slots = slot_ids.reshape(sources, blocks)
+    ref_flat = ref_features.reshape(rows_n * channels, n_cols)
+    warp = functools.partial(variance, slots=slots, disparities=disparities)
+    warp = functools.partial(warp, view_counts=view_counts, arrived=arrived, ref_flat=ref_flat)
+    low, top = warp(((rows_n - 2, rows_n - 1), (0,)))
+    above = passed_along(low, "view", 1)
+    below = passed_along(top, "view", -1)
+    (mid,) = warp((tuple(range(1, rows_n - 2)),))
+    smem = pl.BlockSpec(memory_space=pltpu.SMEM)
+    vmem = pl.BlockSpec(memory_space=pltpu.VMEM)
     first_strip = (lax.axis_index("view") == 0).astype(jnp.int32).reshape(1)
     return pl.pallas_call(
         conv_kernel,
         out_shape=jax.ShapeDtypeStruct((planes // 2, rows_n // 2, c2, half_x), jnp.float32),
-        in_specs=[smem] + [vmem] * 8,
+        in_specs=[smem] + [vmem] * 10,
         out_specs=vmem,
         scratch_shapes=[
             pltpu.VMEM((planes, 3 * part, n_cols), jnp.float32),
             pltpu.VMEM((planes + 1, 3 * part, wide), jnp.bfloat16),
         ],
+        compiler_params=pltpu.CompilerParams(vmem_limit_bytes=24 << 20),
         name="convolutions",
-    )(first_strip, volume, above, below, w1, b1, w2, b2, pick)
+    )(first_strip, above, top, mid, low, below, w1, b1, w2, b2, pick)
 
 
 def solution(mesh):

time: 93.1 us -> 80.5 us (0.86)
  local copies, waits for them, and re-layouts: 36.9 us -> 15.2 us
  waiting for transfers between devices: 13 us -> 24 us
  other arithmetic: 3.35 us -> 1.83 us
    another operation x11 -> x0, local copies, waits for them, and re-layouts: 15.8 us -> none  [banded_first(): return jnp.stack(bands, axis=2).reshape(-1, (rows_n + 3) * channels)]
    all_to_all x1, waiting for transfers between devices: 8.09 us -> 21.7 us  [on_device(): lax.all_to_all(outgoing, 'view', split_axis=0, concat_axis=0, tiled=True)]
    unnamed x31 -> x25, local copies, waits for them, and re-layouts: 10 us -> 1.77 us
    reshape x4, local copies, waits for them, and re-layouts: 0.46 us -> 5.02 us  [banded_second(): bands = [jnp.pad(moved, ((0, 0), (0, 0), (0, 0), (2 * g, rows_n + 2 - tap...]
    ppermute x2, waiting for transfers between devices: 4.92 us -> 2.32 us  [passed_along(): return lax.ppermute(x, axis, pairs)]
    slice x2 -> x0, local copies, waits for them, and re-layouts: 2.04 us -> none  [the longest x1 1.09 us: on_device(): above = passed_along(volume[:, (rows_n - 2) * channels:], 'view', 1)]
    pad x1, local copies, waits for them, and re-layouts: 1.81 us -> 0.73 us  [prepare(): moved = jnp.pad(moved, ((0, 0), (0, 0), (0, lanes - taps_r * channels)))]
    convert_element_type x1 -> x0, other arithmetic: 1.04 us -> none  [on_device(): pick = ((x_in == x_out) & (jnp.arange(wide) < half_x)).astype(jnp.bfloat16)]
  transfers between devices with their start and end apart: 3 -> 3, of which waited for: 2 -> 2; matrix products, arithmetic and copies ran while one was open for 36% -> 15% of each run, Pallas kernels for 0% -> 5%
where the time goes in v2:
time: 80.5 us; the launch traced here: 79.4 us
  waiting for transfers between devices  24 us (30%)
  Pallas kernels  15.6 us (19%)
  local copies, waits for them, and re-layouts  15.2 us (19%)
  starting transfers between devices  11.8 us (15%)
  blocking collectives  10.2 us (13%)
  other arithmetic  1.83 us (2%)
    all_to_all x1, waiting for transfers between devices, on_device(): lax.all_to_all(outgoing, 'view', split_axis=0, concat_axis=0, tiled=True)  21.7 us
    all_to_all x1, blocking collectives, on_device(): lax.all_to_all(wanted, 'view', split_axis=0, concat_axis=0, tiled=True)  10.2 us
    pallas_call x1, Pallas kernels, on_device(): pl.pallas_call(conv_kernel, out_shape=jax.ShapeDtypeStruct((planes // 2,...  8.02 us
    pallas_call x2, Pallas kernels, variance(): pl.pallas_call(functools.partial(variance_kernel, rows), out_shape=[jax.S...  7.26 us
    all_to_all x1, starting transfers between devices, on_device(): lax.all_to_all(outgoing, 'view', split_axis=0, concat_axis=0, tiled=True)  6.35 us
    ppermute x2, starting transfers between devices, passed_along(): return lax.ppermute(x, axis, pairs)  5.46 us
    reshape x4, local copies, waits for them, and re-layouts, banded_second(): bands = [jnp.pad(moved, ((0, 0), (0, 0), (0, 0), (2 * g, rows_n + 2 - tap...  5.02 us
    ppermute x2, waiting for transfers between devices, passed_along(): return lax.ppermute(x, axis, pairs)  2.32 us
  transfers between devices with their start and end apart: 3, of which 2 were waited for; matrix products, arithmetic and copies ran while one was open for 15% of the time, Pallas kernels for 5%

profile of v2, /device:TPU:15, one launch (start us, length us, event | category | flops | bytes accessed | tf_op | source)
XLA Modules:
  0.0 79.4 jit_solution(9703151544565671942)
XLA Ops:
  0.0 0.0 copy-start
  0.0 0.9 %reshape.187 = s32[16]{0:T(128)S(1)} reshape(s32[1,4,4]{2,1,0:T(4,128)} %param.11) | data formatting | bytes 128 | tf_op jit(solution)/shard_map/reshape | solution.py:240
  0.9 0.2 convert_reduce_fusion
  1.1 0.1 select_reduce_fusion
  1.2 0.1 sub.15
  1.3 10.2 %all_to_all.11 = s32[16,1,2]{2,1,0:T(1,128)S(1)} all-to-all(s32[16,1,2]{2,1,0:T(1,128)S(1)} %bitcast.43), channel_id=1, replica_groups=mesh['groups'=2,'view'=16] {'view'}, dimensions={0} | all-to-all | bytes 256 | tf_op jit(solution)/shard_map/all_to_all | solution.py:243
  11.5 0.1 reshape.199
  11.6 0.0 copy-done
  11.6 1.9 %gather_fusion = bf16[32,2,32,384]{3,2,1,0:T(8,128)(2,1)} fusion(bf16[32,2,32,384]{3,2,1,0:T(8,128)(2,1)S(1)} %copy-done, s32[1024]{0:T(1024)S(1)} %pad_clamp_fusion), kind=kCustom, calls=%fused_computation | custom fusion | bytes 3145856 | tf_op jit(solution)/shard_map/gather | solution.py:244
  13.5 0.0 copy-start.10
  13.5 0.0 copy-start.8
  13.5 0.0 copy-start.11
  13.5 0.0 copy-start.6
  13.5 6.3 %all-to-all-start.1 = ((bf16[16,2,2,32,384]{4,3,2,1,0:T(8,128)(2,1)}), bf16[16,2,2,32,384]{4,3,2,1,0:T(8,128)(2,1)S(1)}, u32[]{:S(2)}, u32[]{:S(2)}) async-start(bf16[16,2,2,32,384]{4,3,2,1,0:T(8,128)(2,1)} %bitcast.37), calls=%async_computation.1 | async-start | bytes 3145728 | tf_op jit(solution)/shard_map/all_to_all | solution.py:245
  19.9 0.0 copy-start.1
  19.9 0.7 reduce_sum.21
  21.2 0.0 copy-done.10
  21.2 0.7 broadcast_in_dim.45
  21.9 0.0 copy-done.8
  21.9 0.1 copy.56.disp_ref
  22.0 0.0 copy-done.11
  22.0 0.6 broadcast_in_dim.26
  22.6 0.0 copy-done.6
  22.6 0.7 reshape.189
  23.3 1.8 %fusion.11 = (bf16[16,3,3,10,8]{0,4,3,2,1:T(8,128)(2,1)}, bf16[16,3,3,10,8]{0,4,3,2,1:T(8,128)(2,1)}, bf16[16,3,3,10,8]{0,4,3,2,1:T(8,128)(2,1)}, bf16[16,3,3,10,8]{0,4,3,2,1:T(8,128)(2,1)S(1)}) fusion(bf16[16,3,3,3,8]{0,4,3,2,1:T(8,128)(2,1)} %param.16), kind=kLoop, calls=%fused_computation.34 | loop fusion | bytes 99072 | tf_op jit(solution)/shard_map/jit(_pad)/pad | solution.py:212
  25.1 1.0 %copy.52 = bf16[16,720]{1,0:T(8,128)(2,1)S(1)} copy(bf16[16,720]{0,1:T(8,128)(2,1)} %bitcast.41) | data formatting | bytes 46080 | tf_op jit(solution)/shard_map/reshape | solution.py:214
  26.2 1.7 %copy.55 = bf16[16,720]{1,0:T(8,128)(2,1)} copy(bf16[16,720]{0,1:T(8,128)(2,1)} %bitcast.40) | data formatting | bytes 46080 | tf_op jit(solution)/shard_map/reshape | solution.py:214
  27.8 1.6 %copy.54 = bf16[16,720]{1,0:T(8,128)(2,1)} copy(bf16[16,720]{0,1:T(8,128)(2,1)} %bitcast.39) | data formatting | bytes 46080 | tf_op jit(solution)/shard_map/reshape | solution.py:214
  29.4 0.7 copy.53
  30.2 0.0 copy-start.7
  30.2 0.0 copy-start.9
  30.2 0.7 pad.20.conv_ref
  30.9 0.3 prepare.1
  31.2 0.0 copy-start.2
  31.2 0.8 %copy-done.2 = bf16[384,768]{1,0:T(8,128)(2,1)} copy-done((bf16[384,768]{1,0:T(8,128)(2,1)}, bf16[384,768]{1,0:T(8,128)(2,1)S(1)}, u32[]{:S(2)}) %copy-start.2) | copy-done | bytes 589848
  32.1 0.0 copy-start.4
  32.1 0.8 %copy-done.4 = bf16[720,352]{1,0:T(8,128)(2,1)} copy-done((bf16[720,352]{1,0:T(8,128)(2,1)}, bf16[720,352]{1,0:T(8,128)(2,1)S(1)}, u32[]{:S(2)}) %copy-start.4) | copy-done | bytes 506904
  32.9 0.8 pad_maximum_fusion.w2_ref
  33.7 0.7 fusion.6.slot_ref
  34.4 21.7 %all-to-all-done.1 = bf16[16,2,2,32,384]{4,3,2,1,0:T(8,128)(2,1)S(1)} async-done(((bf16[16,2,2,32,384]{4,3,2,1,0:T(8,128)(2,1)}), bf16[16,2,2,32,384]{4,3,2,1,0:T(8,128)(2,1)S(1)}, u32[]{:S(2)}, u32[]{:S(2)}) %all-to-all-start.1) | async-done | bytes 1572896 | tf_op jit(solution)/shard_map/all_to_all | solution.py:245
  56.1 0.0 copy-done.1
  56.1 3.5 %variance3.1 = (bf16[8,64,384]{2,1,0:T(8,128)(2,1)}, bf16[8,32,384]{2,1,0:T(8,128)(2,1)}) custom-call(s32[4,4]{1,0:T(4,128)S(1)} %fusion.6.slot_ref, s32[8,4]{1,0:T(8,128)S(1)} %copy.56.disp_ref, s32[1]{0:T(128)S(6)} %copy.66.count_ref, bf16[32,64,384]{2,1,0:T(8,128)(2,1)S(1)} %bitcast.33, bf16[256,384]{1,0:T(8,128)(2,1)S(1)} %bitcast.35), custom_call_target="tpu_custom_call" | custom-call | flops 11796480 | bytes 1179648 | tf_op jit(solution)/shard_map/variance3/pallas_call | solution.py:88
  59.6 3.5 %collective-permute-start = (bf16[8,64,384]{2,1,0:T(8,128)(2,1)}, bf16[8,64,384]{2,1,0:T(8,128)(2,1)}, u32[]{:S(2)}, u32[]{:S(2)}) collective-permute-start(bf16[8,64,384]{2,1,0:T(8,128)(2,1)} %get-tuple-element.18.low_ref), channel_id=1, source_target_pairs={{0,1},{1,2},{2,3},{3,4},{4,5},{5,6},{6,7},{7,8},{8,9},{9,10},{10,1... | collective-permute-start | bytes 1179656 | tf_op jit(solution)/shard_map/ppermute | solution.py:14
  63.2 1.9 %collective-permute-start.1 = (bf16[8,32,384]{2,1,0:T(8,128)(2,1)}, bf16[8,32,384]{2,1,0:T(8,128)(2,1)}, u32[]{:S(2)}, u32[]{:S(2)}) collective-permute-start(bf16[8,32,384]{2,1,0:T(8,128)(2,1)} %get-tuple-element.19.top_ref), channel_id=1, source_target_pairs={{1,0},{2,1},{3,2},{4,3},{5,4},{6,5},{7,6},{8,7},{9,8},{10,9},{11,1... | collective-permute-start | bytes 589832 | tf_op jit(solution)/shard_map/ppermute | solution.py:14
  65.1 0.0 copy-done.7
  65.1 0.1 copy.59.b2_ref
  65.2 0.0 copy-done.9
  65.2 0.1 copy.58.b1_ref
  65.3 0.0 copy-start.3
  65.3 0.0 copy-start.5
  65.3 3.7 %variance5.1.mid_ref = bf16[8,160,384]{2,1,0:T(8,128)(2,1)S(1)} custom-call(s32[4,4]{1,0:T(4,128)S(1)} %fusion.6.slot_ref, s32[8,4]{1,0:T(8,128)S(1)} %copy.56.disp_ref, s32[1]{0:T(128)S(6)} %copy.66.count_ref, bf16[32,64,384]{2,1,0:T(8,128)(2,1)S(1)} %bitcast.34, bf16[256,384]{1,0:T(8,128)(2,1)S(1)} %bitcast.36), custom_call_target="tpu_custom_call" | custom-call | flops 19660800 | bytes 1966080 | tf_op jit(solution)/shard_map/variance5/pallas_call | solution.py:88
  69.1 2.3 %collective-permute-done.1.below_ref = bf16[8,32,384]{2,1,0:T(8,128)(2,1)} collective-permute-done((bf16[8,32,384]{2,1,0:T(8,128)(2,1)}, bf16[8,32,384]{2,1,0:T(8,128)(2,1)}, u32[]{:S(2)}, u32[]{:S(2)}) %collective-permute-start.1) | collective-permute-done | bytes 196640 | tf_op jit(solution)/shard_map/ppermute | solution.py:14
  71.4 0.0 collective-permute-done.above_ref
  71.4 0.0 copy-done.3
  71.4 0.0 copy-done.5
  71.4 8.0 %convolutions.1 = f32[4,4,16,192]{3,2,1,0:T(8,128)} custom-call(s32[1]{0:T(128)} %bitcast.first_strip_ref, bf16[8,64,384]{2,1,0:T(8,128)(2,1)} %collective-permute-done.above_ref, bf16[8,32,384]{2,1,0:T(8,128)(2,1)} %get-tuple-element.19.top_ref, bf16[8,160,384]{2,1,0:T(8,128)(2,1)S(1)} %variance5.1.mid_ref, bf16[8,64,384]{2,1,0:T(8,128)(2,1)} %get-tuple-element.18.low_ref, ...), custom_call_target="tpu_custom_call" | custom-call | tf_op jit(solution)/shard_map/convolutions/pallas_call | solution.py:267
  (9 shorter events, 0.1 us)
Async XLA Ops:
  0.0 11.6 %copy-start = (bf16[32,2,32,384]{3,2,1,0:T(8,128)(2,1)S(1)}, bf16[32,2,32,384]{3,2,1,0:T(8,128)(2,1)}, u32[]{:S(2)}) copy-start(bf16[32,2,32,384]{3,2,1,0:T(8,128)(2,1)} %param.10) | copy-start | bytes 4718596
  13.5 7.7 %copy-start.10 = (f32[16]{0:T(128)S(1)}, f32[16]{0:T(128)}, u32[]{:S(2)}) copy-start(f32[16]{0:T(128)} %param.17) | copy-start | bytes 196
  13.5 8.4 %copy-start.8 = (s32[8,4]{0,1:T(4,128)S(1)}, s32[8,4]{0,1:T(4,128)}, u32[]{:S(2)}) copy-start(s32[8,4]{0,1:T(4,128)} %param.13) | copy-start | bytes 388
  13.5 8.4 %copy-start.11 = (f32[8]{0:T(128)S(1)}, f32[8]{0:T(128)}, u32[]{:S(2)}) copy-start(f32[8]{0:T(128)} %param.15) | copy-start | bytes 100
  13.5 9.1 %copy-start.6 = (bf16[3,3,8,3,32]{4,2,3,1,0:T(8,128)(2,1)S(1)}, bf16[3,3,8,3,32]{4,2,3,1,0:T(8,128)(2,1)}, u32[]{:S(2)}) copy-start(bf16[3,3,8,3,32]{4,2,3,1,0:T(8,128)(2,1)} %param.14) | copy-start | bytes 41476
  13.5 42.5 %all-to-all-start.1 = ((bf16[16,2,2,32,384]{4,3,2,1,0:T(8,128)(2,1)}), bf16[16,2,2,32,384]{4,3,2,1,0:T(8,128)(2,1)S(1)}, u32[]{:S(2)}, u32[]{:S(2)}) async-start(bf16[16,2,2,32,384]{4,3,2,1,0:T(8,128)(2,1)} %bitcast.37), calls=%async_computation.1 | async-start | bytes 3145728 | tf_op jit(solution)/shard_map/all_to_all | solution.py:245
  19.9 36.2 %copy-start.1 = (bf16[8,32,384]{2,1,0:T(8,128)(2,1)S(1)}, bf16[8,32,384]{2,1,0:T(8,128)(2,1)}, u32[]{:S(2)}) copy-start(bf16[8,32,384]{2,1,0:T(8,128)(2,1)} %param.9) | copy-start | bytes 589828
  30.2 34.9 %copy-start.7 = (f32[64,1]{0,1:T(1,128)S(1)}, f32[64,1]{0,1:T(1,128)}, u32[]{:S(2)}) copy-start(f32[64,1]{0,1:T(1,128)} %broadcast_in_dim.45) | copy-start | bytes 772
  30.2 35.1 %copy-start.9 = (f32[80,1]{0,1:T(1,128)S(1)}, f32[80,1]{0,1:T(1,128)}, u32[]{:S(2)}) copy-start(f32[80,1]{0,1:T(1,128)} %broadcast_in_dim.26) | copy-start | bytes 964
  31.2 0.8 %copy-start.2 = (bf16[384,768]{1,0:T(8,128)(2,1)}, bf16[384,768]{1,0:T(8,128)(2,1)S(1)}, u32[]{:S(2)}) copy-start(bf16[384,768]{1,0:T(8,128)(2,1)S(1)} %get-tuple-element.24.pick_ref) | copy-start | bytes 1769476
  32.1 0.8 %copy-start.4 = (bf16[720,352]{1,0:T(8,128)(2,1)}, bf16[720,352]{1,0:T(8,128)(2,1)S(1)}, u32[]{:S(2)}) copy-start(bf16[720,352]{1,0:T(8,128)(2,1)S(1)} %get-tuple-element.20.w1_ref) | copy-start | bytes 1520644
  59.6 11.8 %collective-permute-start = (bf16[8,64,384]{2,1,0:T(8,128)(2,1)}, bf16[8,64,384]{2,1,0:T(8,128)(2,1)}, u32[]{:S(2)}, u32[]{:S(2)}) collective-permute-start(bf16[8,64,384]{2,1,0:T(8,128)(2,1)} %get-tuple-element.18.low_ref), channel_id=1, source_target_pairs={{0,1},{1,2},{2,3},{3,4},{4,5},{5,6},{6,7},{7,8},{8,9},{9,10},{10,1... | collective-permute-start | bytes 1179656 | tf_op jit(solution)/shard_map/ppermute | solution.py:14
  63.2 8.2 %collective-permute-start.1 = (bf16[8,32,384]{2,1,0:T(8,128)(2,1)}, bf16[8,32,384]{2,1,0:T(8,128)(2,1)}, u32[]{:S(2)}, u32[]{:S(2)}) collective-permute-start(bf16[8,32,384]{2,1,0:T(8,128)(2,1)} %get-tuple-element.19.top_ref), channel_id=1, source_target_pairs={{1,0},{2,1},{3,2},{4,3},{5,4},{6,5},{7,6},{8,7},{9,8},{10,9},{11,1... | collective-permute-start | bytes 589832 | tf_op jit(solution)/shard_map/ppermute | solution.py:14
  65.3 6.1 %copy-start.3 = (bf16[384,768]{1,0:T(8,128)(2,1)S(1)}, bf16[384,768]{1,0:T(8,128)(2,1)}, u32[]{:S(2)}) copy-start(bf16[384,768]{1,0:T(8,128)(2,1)} %copy-done.2) | copy-start | bytes 1769476
  65.3 6.1 %copy-start.5 = (bf16[720,352]{1,0:T(8,128)(2,1)S(1)}, bf16[720,352]{1,0:T(8,128)(2,1)}, u32[]{:S(2)}) copy-start(bf16[720,352]{1,0:T(8,128)(2,1)} %copy-done.4) | copy-start | bytes 1520644

commit v3 on v2

--- a/solution.py
+++ b/solution.py
@@ -30,6 +30,71 @@
     matches = slot_ids[:, None] == positions[None, :]
     wanted = jnp.sum(jnp.where(matches, local_ids[:, None] + 1, 0), axis=0) - 1
     return wanted.reshape(n_view, slot_cap)
+
+
+def ask_kernel(n_view, wanted_ref, asked_ref, send_sem, recv_sem):
+    me = lax.axis_index("view")
+    mesh_id = pl.DeviceIdType.MESH
+    barrier = pltpu.get_barrier_semaphore()
+
+    def greet(step, carry):
+        peer = lax.rem(me + step, n_view)
+        pl.semaphore_signal(barrier, inc=1, device_id={"view": peer}, device_id_type=mesh_id)
+        return carry
+
+    lax.fori_loop(1, n_view, greet, 0)
+    pl.semaphore_wait(barrier, n_view - 1)
+
+    def ask(step, carry):
+        peer = lax.rem(me + step, n_view)
+        pltpu.make_async_remote_copy(
+            src_ref=wanted_ref.at[peer],
+            dst_ref=asked_ref.at[me],
+            send_sem=send_sem.at[peer],
+            recv_sem=recv_sem.at[me],
+            device_id={"view": peer},
+            device_id_type=mesh_id,
+        ).start()
+        return carry
+
+    lax.fori_loop(1, n_view, ask, 0)
+    asked_ref[me] = wanted_ref[me]
+
+    def settle(step, carry):
+        peer = lax.rem(me + step, n_view)
+        copy = pltpu.make_async_remote_copy(
+            src_ref=wanted_ref.at[peer],
+            dst_ref=asked_ref.at[peer],
+            send_sem=send_sem.at[peer],
+            recv_sem=recv_sem.at[peer],
+            device_id={"view": peer},
+            device_id_type=mesh_id,
+        )
+        copy.wait_send()
+        copy.wait_recv()
+        return carry
+
+    lax.fori_loop(1, n_view, settle, 0)
+
+
+def ask_owners(wanted):
+    n_view, slot_cap = wanted.shape
+    table = jnp.broadcast_to(
+        jnp.pad(wanted, ((0, 0), (0, 128 - slot_cap)))[:, None, :], (n_view, 8, 128)
+    )
+    vmem = pl.BlockSpec(memory_space=pltpu.VMEM)
+    asked = pl.pallas_call(
+        functools.partial(ask_kernel, n_view),
+        out_shape=jax.ShapeDtypeStruct(table.shape, jnp.int32),
+        in_specs=[vmem],
+        out_specs=vmem,
+        scratch_shapes=[pltpu.SemaphoreType.DMA((n_view,)), pltpu.SemaphoreType.DMA((n_view,))],
+        compiler_params=pltpu.CompilerParams(
+            collective_id=0, has_side_effects=True, vmem_limit_bytes=4 << 20
+        ),
+        name="ask",
+    )(table)
+    return asked[:, 0, :slot_cap]
 
 
 def variance_kernel(rows, slot_ref, disp_ref, count_ref, arrived_ref, ref_ref, *refs):
@@ -240,7 +305,7 @@
     flat_ids = pair_lists.reshape(request_total)
     slot_ids, local_ids = request_slots(flat_ids, slot_cap, tiles_dev)
     wanted = request_table(slot_ids, local_ids, n_view, slot_cap)
-    asked = lax.all_to_all(wanted, "view", split_axis=0, concat_axis=0, tiled=True)
+    asked = ask_owners(wanted)
     outgoing = source_tiles[jnp.maximum(asked, 0)]
     arrived = lax.all_to_all(outgoing, "view", split_axis=0, concat_axis=0, tiled=True)
     arrived = arrived.reshape(n_view * slot_cap, 2 * channels, n_cols)

time: 80.5 us -> 77.8 us (0.966)
  blocking collectives: 10.2 us -> 0 us
  Pallas kernels: 15.6 us -> 22.9 us
    all_to_all x1 -> x0, blocking collectives: 10.2 us -> none  [on_device(): lax.all_to_all(wanted, 'view', split_axis=0, concat_axis=0, tiled=True)]
    pallas_call x0 -> x1, Pallas kernels: none -> 7.31 us  [ask_owners(): pl.pallas_call(functools.partial(ask_kernel, n_view), out_shape=jax.Shape...]
  transfers between devices with their start and end apart: 3 -> 3, of which waited for: 2 -> 2; matrix products, arithmetic and copies ran while one was open for 15% -> 16% of each run, Pallas kernels for 5% -> 5%
where the time goes in v3:
time: 77.8 us; the launch traced here: 76.8 us
  waiting for transfers between devices  24 us (31%)
  Pallas kernels  22.9 us (29%)
  local copies, waits for them, and re-layouts  15.2 us (20%)
  starting transfers between devices  12 us (15%)
  other arithmetic  1.83 us (2%)
  between operations  0.83 us (1%)
    all_to_all x1, waiting for transfers between devices, on_device(): lax.all_to_all(outgoing, 'view', split_axis=0, concat_axis=0, tiled=True)  21.7 us
    pallas_call x1, Pallas kernels, on_device(): pl.pallas_call(conv_kernel, out_shape=jax.ShapeDtypeStruct((planes // 2,...  8.02 us
    pallas_call x1, Pallas kernels, ask_owners(): pl.pallas_call(functools.partial(ask_kernel, n_view), out_shape=jax.Shape...  7.31 us
    pallas_call x2, Pallas kernels, variance(): pl.pallas_call(functools.partial(variance_kernel, rows), out_shape=[jax.S...  7.26 us
    all_to_all x1, starting transfers between devices, on_device(): lax.all_to_all(outgoing, 'view', split_axis=0, concat_axis=0, tiled=True)  6.54 us
    ppermute x2, starting transfers between devices, passed_along(): return lax.ppermute(x, axis, pairs)  5.48 us
    reshape x4, local copies, waits for them, and re-layouts, banded_second(): bands = [jnp.pad(moved, ((0, 0), (0, 0), (0, 0), (2 * g, rows_n + 2 - tap...  5.02 us
    ppermute x2, waiting for transfers between devices, passed_along(): return lax.ppermute(x, axis, pairs)  2.32 us
  transfers between devices with their start and end apart: 3, of which 2 were waited for; matrix products, arithmetic and copies ran while one was open for 16% of the time, Pallas kernels for 5%

profile of v3, /device:TPU:15, one launch (start us, length us, event | category | flops | bytes accessed | tf_op | source)
XLA Modules:
  0.0 76.8 jit_solution(4624171256662630212)
XLA Ops:
  0.0 0.0 copy-start
  0.0 0.9 %reshape.176 = s32[16]{0:T(128)S(1)} reshape(s32[1,4,4]{2,1,0:T(4,128)} %param.11) | data formatting | bytes 128 | tf_op jit(solution)/shard_map/reshape | solution.py:305
  0.9 0.2 convert_reduce_fusion
  1.1 0.1 select_reduce_fusion
  1.2 0.1 sub.15
  1.3 7.3 %ask.1 = s32[16,8,128]{2,1,0:T(8,128)S(1)} custom-call(s32[16,8,128]{2,1,0:T(8,128)S(1)} %broadcast_in_dim.27.wanted_ref), custom_call_target="tpu_custom_call" | custom-call | tf_op jit(solution)/shard_map/ask/pallas_call | solution.py:86
  8.7 0.1 reshape.188
  8.8 0.0 copy-done
  8.8 1.9 %gather_fusion = bf16[32,2,32,384]{3,2,1,0:T(8,128)(2,1)} fusion(bf16[32,2,32,384]{3,2,1,0:T(8,128)(2,1)S(1)} %copy-done, s32[1024]{0:T(1024)S(1)} %pad_clamp_fusion), kind=kCustom, calls=%fused_computation | custom fusion | bytes 3145856 | tf_op jit(solution)/shard_map/gather | solution.py:309
  10.7 0.0 copy-start.10
  10.7 0.0 copy-start.8
  10.7 0.0 copy-start.11
  10.7 0.0 copy-start.6
  10.7 6.5 %all-to-all-start = ((bf16[16,2,2,32,384]{4,3,2,1,0:T(8,128)(2,1)}), bf16[16,2,2,32,384]{4,3,2,1,0:T(8,128)(2,1)S(1)}, u32[]{:S(2)}, u32[]{:S(2)}) async-start(bf16[16,2,2,32,384]{4,3,2,1,0:T(8,128)(2,1)} %bitcast.36), calls=%async_computation | async-start | bytes 3145728 | tf_op jit(solution)/shard_map/all_to_all | solution.py:310
  17.2 0.0 copy-start.1
  17.3 0.7 reduce_sum.21
  18.6 0.0 copy-done.10
  18.6 0.7 broadcast_in_dim.52
  19.2 0.0 copy-done.8
  19.2 0.1 copy.41.disp_ref
  19.3 0.0 copy-done.11
  19.3 0.6 broadcast_in_dim.29
  19.9 0.0 copy-done.6
  20.0 0.7 reshape.178
  20.7 1.8 %fusion.11 = (bf16[16,3,3,10,8]{0,4,3,2,1:T(8,128)(2,1)}, bf16[16,3,3,10,8]{0,4,3,2,1:T(8,128)(2,1)}, bf16[16,3,3,10,8]{0,4,3,2,1:T(8,128)(2,1)}, bf16[16,3,3,10,8]{0,4,3,2,1:T(8,128)(2,1)S(1)}) fusion(bf16[16,3,3,3,8]{0,4,3,2,1:T(8,128)(2,1)} %param.16), kind=kLoop, calls=%fused_computation.34 | loop fusion | bytes 99072 | tf_op jit(solution)/shard_map/jit(_pad)/pad | solution.py:277
  22.5 1.0 %copy.37 = bf16[16,720]{1,0:T(8,128)(2,1)S(1)} copy(bf16[16,720]{0,1:T(8,128)(2,1)} %bitcast.40) | data formatting | bytes 46080 | tf_op jit(solution)/shard_map/reshape | solution.py:279
  23.5 1.7 %copy.40 = bf16[16,720]{1,0:T(8,128)(2,1)} copy(bf16[16,720]{0,1:T(8,128)(2,1)} %bitcast.39) | data formatting | bytes 46080 | tf_op jit(solution)/shard_map/reshape | solution.py:279
  25.2 1.6 %copy.39 = bf16[16,720]{1,0:T(8,128)(2,1)} copy(bf16[16,720]{0,1:T(8,128)(2,1)} %bitcast.38) | data formatting | bytes 46080 | tf_op jit(solution)/shard_map/reshape | solution.py:279
  26.8 0.7 copy.38
  27.5 0.0 copy-start.7
  27.5 0.0 copy-start.9
  27.5 0.7 pad.25.conv_ref
  28.3 0.3 prepare.1
  28.6 0.0 copy-start.2
  28.6 0.8 %copy-done.2 = bf16[384,768]{1,0:T(8,128)(2,1)} copy-done((bf16[384,768]{1,0:T(8,128)(2,1)}, bf16[384,768]{1,0:T(8,128)(2,1)S(1)}, u32[]{:S(2)}) %copy-start.2) | copy-done | bytes 589848
  29.4 0.0 copy-start.4
  29.4 0.8 %copy-done.4 = bf16[720,352]{1,0:T(8,128)(2,1)} copy-done((bf16[720,352]{1,0:T(8,128)(2,1)}, bf16[720,352]{1,0:T(8,128)(2,1)S(1)}, u32[]{:S(2)}) %copy-start.4) | copy-done | bytes 506904
  30.2 0.8 %pad_maximum_fusion.w2_ref = bf16[64,720]{1,0:T(8,128)(2,1)S(1)} fusion(bf16[16,720]{1,0:T(8,128)(2,1)} %copy.40, bf16[16,720]{1,0:T(8,128)(2,1)} %copy.39, bf16[16,720]{1,0:T(8,128)(2,1)} %copy.38, bf16[16,720]{1,0:T(8,128)(2,1)S(1)} %copy.37), kind=kLoop, calls=%fused_computation.1 | loop fusion | flops 368640 | bytes 184320 | tf_op jit(solution)/shard_map/concatenate | solution.py:282
  31.0 0.7 fusion.6.slot_ref
  31.7 21.7 %all-to-all-done = bf16[16,2,2,32,384]{4,3,2,1,0:T(8,128)(2,1)S(1)} async-done(((bf16[16,2,2,32,384]{4,3,2,1,0:T(8,128)(2,1)}), bf16[16,2,2,32,384]{4,3,2,1,0:T(8,128)(2,1)S(1)}, u32[]{:S(2)}, u32[]{:S(2)}) %all-to-all-start) | async-done | bytes 1572896 | tf_op jit(solution)/shard_map/all_to_all | solution.py:310
  53.4 0.0 copy-done.1
  53.4 3.5 %variance3.1 = (bf16[8,64,384]{2,1,0:T(8,128)(2,1)}, bf16[8,32,384]{2,1,0:T(8,128)(2,1)}) custom-call(s32[4,4]{1,0:T(4,128)S(1)} %fusion.6.slot_ref, s32[8,4]{1,0:T(8,128)S(1)} %copy.41.disp_ref, s32[1]{0:T(128)S(6)} %copy.51.count_ref, bf16[32,64,384]{2,1,0:T(8,128)(2,1)S(1)} %bitcast.32, bf16[256,384]{1,0:T(8,128)(2,1)S(1)} %bitcast.34), custom_call_target="tpu_custom_call" | custom-call | flops 11796480 | bytes 1179648 | tf_op jit(solution)/shard_map/variance3/pallas_call | solution.py:153
  57.0 3.6 %collective-permute-start = (bf16[8,64,384]{2,1,0:T(8,128)(2,1)}, bf16[8,64,384]{2,1,0:T(8,128)(2,1)}, u32[]{:S(2)}, u32[]{:S(2)}) collective-permute-start(bf16[8,64,384]{2,1,0:T(8,128)(2,1)} %get-tuple-element.18.low_ref), channel_id=1, source_target_pairs={{0,1},{1,2},{2,3},{3,4},{4,5},{5,6},{6,7},{7,8},{8,9},{9,10},{10,1... | collective-permute-start | bytes 1179656 | tf_op jit(solution)/shard_map/ppermute | solution.py:14
  60.5 1.9 %collective-permute-start.1 = (bf16[8,32,384]{2,1,0:T(8,128)(2,1)}, bf16[8,32,384]{2,1,0:T(8,128)(2,1)}, u32[]{:S(2)}, u32[]{:S(2)}) collective-permute-start(bf16[8,32,384]{2,1,0:T(8,128)(2,1)} %get-tuple-element.19.top_ref), channel_id=1, source_target_pairs={{1,0},{2,1},{3,2},{4,3},{5,4},{6,5},{7,6},{8,7},{9,8},{10,9},{11,1... | collective-permute-start | bytes 589832 | tf_op jit(solution)/shard_map/ppermute | solution.py:14
  62.5 0.0 copy-done.7
  62.5 0.1 copy.44.b2_ref
  62.6 0.0 copy-done.9
  62.6 0.1 copy.43.b1_ref
  62.7 0.0 copy-start.3
  62.7 0.0 copy-start.5
  62.7 3.7 %variance5.1.mid_ref = bf16[8,160,384]{2,1,0:T(8,128)(2,1)S(1)} custom-call(s32[4,4]{1,0:T(4,128)S(1)} %fusion.6.slot_ref, s32[8,4]{1,0:T(8,128)S(1)} %copy.41.disp_ref, s32[1]{0:T(128)S(6)} %copy.51.count_ref, bf16[32,64,384]{2,1,0:T(8,128)(2,1)S(1)} %bitcast.33, bf16[256,384]{1,0:T(8,128)(2,1)S(1)} %bitcast.35), custom_call_target="tpu_custom_call" | custom-call | flops 19660800 | bytes 1966080 | tf_op jit(solution)/shard_map/variance5/pallas_call | solution.py:153
  66.4 2.3 %collective-permute-done.1.below_ref = bf16[8,32,384]{2,1,0:T(8,128)(2,1)} collective-permute-done((bf16[8,32,384]{2,1,0:T(8,128)(2,1)}, bf16[8,32,384]{2,1,0:T(8,128)(2,1)}, u32[]{:S(2)}, u32[]{:S(2)}) %collective-permute-start.1) | collective-permute-done | bytes 196640 | tf_op jit(solution)/shard_map/ppermute | solution.py:14
  68.7 0.0 collective-permute-done.above_ref
  68.7 0.0 copy-done.3
  68.7 0.0 copy-done.5
  68.7 8.0 %convolutions.1 = f32[4,4,16,192]{3,2,1,0:T(8,128)} custom-call(s32[1]{0:T(128)} %bitcast.first_strip_ref, bf16[8,64,384]{2,1,0:T(8,128)(2,1)} %collective-permute-done.above_ref, bf16[8,32,384]{2,1,0:T(8,128)(2,1)} %get-tuple-element.19.top_ref, bf16[8,160,384]{2,1,0:T(8,128)(2,1)S(1)} %variance5.1.mid_ref, bf16[8,64,384]{2,1,0:T(8,128)(2,1)} %get-tuple-element.18.low_ref, ...), custom_call_target="tpu_custom_call" | custom-call | tf_op jit(solution)/shard_map/convolutions/pallas_call | solution.py:332
  (11 shorter events, 0.1 us)
Async XLA Ops:
  0.0 8.8 %copy-start = (bf16[32,2,32,384]{3,2,1,0:T(8,128)(2,1)S(1)}, bf16[32,2,32,384]{3,2,1,0:T(8,128)(2,1)}, u32[]{:S(2)}) copy-start(bf16[32,2,32,384]{3,2,1,0:T(8,128)(2,1)} %param.10) | copy-start | bytes 4718596
  10.7 7.9 %copy-start.10 = (f32[16]{0:T(128)S(1)}, f32[16]{0:T(128)}, u32[]{:S(2)}) copy-start(f32[16]{0:T(128)} %param.17) | copy-start | bytes 196
  10.7 8.6 %copy-start.8 = (s32[8,4]{0,1:T(4,128)S(1)}, s32[8,4]{0,1:T(4,128)}, u32[]{:S(2)}) copy-start(s32[8,4]{0,1:T(4,128)} %param.13) | copy-start | bytes 388
  10.7 8.6 %copy-start.11 = (f32[8]{0:T(128)S(1)}, f32[8]{0:T(128)}, u32[]{:S(2)}) copy-start(f32[8]{0:T(128)} %param.15) | copy-start | bytes 100
  10.7 9.2 %copy-start.6 = (bf16[3,3,8,3,32]{4,2,3,1,0:T(8,128)(2,1)S(1)}, bf16[3,3,8,3,32]{4,2,3,1,0:T(8,128)(2,1)}, u32[]{:S(2)}) copy-start(bf16[3,3,8,3,32]{4,2,3,1,0:T(8,128)(2,1)} %param.14) | copy-start | bytes 41476
  10.7 42.7 %all-to-all-start = ((bf16[16,2,2,32,384]{4,3,2,1,0:T(8,128)(2,1)}), bf16[16,2,2,32,384]{4,3,2,1,0:T(8,128)(2,1)S(1)}, u32[]{:S(2)}, u32[]{:S(2)}) async-start(bf16[16,2,2,32,384]{4,3,2,1,0:T(8,128)(2,1)} %bitcast.36), calls=%async_computation | async-start | bytes 3145728 | tf_op jit(solution)/shard_map/all_to_all | solution.py:310
  17.2 36.2 %copy-start.1 = (bf16[8,32,384]{2,1,0:T(8,128)(2,1)S(1)}, bf16[8,32,384]{2,1,0:T(8,128)(2,1)}, u32[]{:S(2)}) copy-start(bf16[8,32,384]{2,1,0:T(8,128)(2,1)} %param.9) | copy-start | bytes 589828
  27.5 34.9 %copy-start.7 = (f32[64,1]{0,1:T(1,128)S(1)}, f32[64,1]{0,1:T(1,128)}, u32[]{:S(2)}) copy-start(f32[64,1]{0,1:T(1,128)} %broadcast_in_dim.52) | copy-start | bytes 772
  27.5 35.1 %copy-start.9 = (f32[80,1]{0,1:T(1,128)S(1)}, f32[80,1]{0,1:T(1,128)}, u32[]{:S(2)}) copy-start(f32[80,1]{0,1:T(1,128)} %broadcast_in_dim.29) | copy-start | bytes 964
  28.6 0.8 %copy-start.2 = (bf16[384,768]{1,0:T(8,128)(2,1)}, bf16[384,768]{1,0:T(8,128)(2,1)S(1)}, u32[]{:S(2)}) copy-start(bf16[384,768]{1,0:T(8,128)(2,1)S(1)} %get-tuple-element.24.pick_ref) | copy-start | bytes 1769476
  29.4 0.8 %copy-start.4 = (bf16[720,352]{1,0:T(8,128)(2,1)}, bf16[720,352]{1,0:T(8,128)(2,1)S(1)}, u32[]{:S(2)}) copy-start(bf16[720,352]{1,0:T(8,128)(2,1)S(1)} %get-tuple-element.20.w1_ref) | copy-start | bytes 1520644
  57.0 11.8 %collective-permute-start = (bf16[8,64,384]{2,1,0:T(8,128)(2,1)}, bf16[8,64,384]{2,1,0:T(8,128)(2,1)}, u32[]{:S(2)}, u32[]{:S(2)}) collective-permute-start(bf16[8,64,384]{2,1,0:T(8,128)(2,1)} %get-tuple-element.18.low_ref), channel_id=1, source_target_pairs={{0,1},{1,2},{2,3},{3,4},{4,5},{5,6},{6,7},{7,8},{8,9},{9,10},{10,1... | collective-permute-start | bytes 1179656 | tf_op jit(solution)/shard_map/ppermute | solution.py:14
  60.5 8.2 %collective-permute-start.1 = (bf16[8,32,384]{2,1,0:T(8,128)(2,1)}, bf16[8,32,384]{2,1,0:T(8,128)(2,1)}, u32[]{:S(2)}, u32[]{:S(2)}) collective-permute-start(bf16[8,32,384]{2,1,0:T(8,128)(2,1)} %get-tuple-element.19.top_ref), channel_id=1, source_target_pairs={{1,0},{2,1},{3,2},{4,3},{5,4},{6,5},{7,6},{8,7},{9,8},{10,9},{11,1... | collective-permute-start | bytes 589832 | tf_op jit(solution)/shard_map/ppermute | solution.py:14
  62.7 6.1 %copy-start.3 = (bf16[384,768]{1,0:T(8,128)(2,1)S(1)}, bf16[384,768]{1,0:T(8,128)(2,1)}, u32[]{:S(2)}) copy-start(bf16[384,768]{1,0:T(8,128)(2,1)} %copy-done.2) | copy-start | bytes 1769476
  62.7 6.1 %copy-start.5 = (bf16[720,352]{1,0:T(8,128)(2,1)S(1)}, bf16[720,352]{1,0:T(8,128)(2,1)}, u32[]{:S(2)}) copy-start(bf16[720,352]{1,0:T(8,128)(2,1)} %copy-done.4) | copy-start | bytes 1520644

commit v4 on v3

--- a/solution.py
+++ b/solution.py
@@ -171,16 +171,13 @@
     groups, c1, n_lanes = conv_ref.shape
     rows_out = w1_ref.shape[0] // (groups * c1)
     width = w1_ref.shape[1]
-    channels = width // (rows_out + 1)
+    channels = width // (rows_out + 2)
+    bands = []
     for group in range(groups):
         base = conv_ref[group].astype(jnp.float32)
-        pieces = [
-            pltpu.roll(base, hi * channels, 1) if hi else base for hi in range(rows_out - 1)
-        ]
-        pieces.append(jnp.zeros_like(base))
-        band = jnp.concatenate(pieces, axis=0).astype(jnp.bfloat16)
-        size = rows_out * c1
-        w1_ref[group * size : (group + 1) * size] = band[:, :width]
+        for hi in range(rows_out):
+            bands.append(pltpu.roll(base, hi * channels, 1) if hi else base)
+    w1_ref[...] = jnp.concatenate(bands, axis=0).astype(jnp.bfloat16)[:, :width]
     n_cols = pick_ref.shape[0]
     wide = pick_ref.shape[1] // 3
     source = lax.broadcasted_iota(jnp.int32, (n_cols, wide), 0)
@@ -195,7 +192,9 @@
     out_ref, acc_ref, cost_ref,
 ):
     planes, _, n_cols = mid_ref.shape
-    part = w1_ref.shape[0] // 9
+    half = w1_ref.shape[0] // 9
+    part = 2 * half
+    depth = w1_ref.shape[1]
     half_p, half_r, c2, half_x = out_ref.shape
     wide = pick_ref.shape[1] // 3
     weights = w1_ref[...]
@@ -203,15 +202,24 @@
     def one_plane(plane):
         strips = (above_ref, top_ref, mid_ref, low_ref, below_ref)
         block = jnp.concatenate([strip[plane] for strip in strips], axis=0)
-        product = jnp.dot(weights, block, preferred_element_type=jnp.float32)
+        skip = depth // (half_r + 3) * (half_r + 1)
+        lower = block[skip:]
+        products = (
+            jnp.dot(weights, block[:depth], preferred_element_type=jnp.float32),
+            jnp.dot(weights[:, : lower.shape[0]], lower, preferred_element_type=jnp.float32),
+        )
         for tap in range(3):
             target = plane + 1 - tap
             if 0 <= target < planes:
-                piece = product[tap * 3 * part : (tap + 1) * 3 * part]
-                if tap == 0 or (tap == 1 and plane == 0):
-                    acc_ref[target] = piece
-                else:
-                    acc_ref[target] += piece
+                for shift in range(3):
+                    for side in range(2):
+                        start = (tap * 3 + shift) * half
+                        piece = products[side][start : start + half]
+                        at = slice(shift * part + side * half, shift * part + (side + 1) * half)
+                        if tap == 0 or (tap == 1 and plane == 0):
+                            acc_ref[target, at] = piece
+                        else:
+                            acc_ref[target, at] += piece
 
     column = lax.broadcasted_iota(jnp.int32, (part, n_cols), 1)
     row = lax.broadcasted_iota(jnp.int32, (part, n_cols), 0)
@@ -250,7 +258,8 @@
 
 def prepare(conv_first, rows_n, n_cols, wide):
     taps_p, taps_r, c1, taps_x, channels = conv_first.shape
-    width = (rows_n + 3) * channels
+    half_rows = (rows_n + 2) // 2
+    width = (half_rows + 2) * channels
     lanes = -(-width // 128) * 128
     groups = taps_p * taps_x
     moved = jnp.transpose(conv_first, (0, 3, 2, 1, 4)).reshape(groups, c1, taps_r * channels)
@@ -259,7 +268,7 @@
     return pl.pallas_call(
         prepare_kernel,
         out_shape=[
-            jax.ShapeDtypeStruct((groups * (rows_n + 2) * c1, width), jnp.bfloat16),
+            jax.ShapeDtypeStruct((groups * half_rows * c1, width), jnp.bfloat16),
             jax.ShapeDtypeStruct((n_cols, 3 * wide), jnp.bfloat16),
         ],
         in_specs=[vmem],

time: 77.8 us -> 76.4 us (0.982)
  Pallas kernels: 22.9 us -> 21.4 us
    pallas_call x1, Pallas kernels: 8.02 us -> 6.58 us  [on_device(): pl.pallas_call(conv_kernel, out_shape=jax.ShapeDtypeStruct((planes // 2,...]
where the time goes in v4:
time: 76.4 us; the launch traced here: 75.3 us
  waiting for transfers between devices  24.3 us (32%)
  Pallas kernels  21.4 us (28%)
  local copies, waits for them, and re-layouts  15 us (20%)
  starting transfers between devices  12 us (16%)
  other arithmetic  1.83 us (2%)
  between operations  0.83 us (1%)
    all_to_all x1, waiting for transfers between devices, on_device(): lax.all_to_all(outgoing, 'view', split_axis=0, concat_axis=0, tiled=True)  21.9 us
    pallas_call x1, Pallas kernels, ask_owners(): pl.pallas_call(functools.partial(ask_kernel, n_view), out_shape=jax.Shape...  7.31 us
    pallas_call x2, Pallas kernels, variance(): pl.pallas_call(functools.partial(variance_kernel, rows), out_shape=[jax.S...  7.26 us
    pallas_call x1, Pallas kernels, on_device(): pl.pallas_call(conv_kernel, out_shape=jax.ShapeDtypeStruct((planes // 2,...  6.58 us
    all_to_all x1, starting transfers between devices, on_device(): lax.all_to_all(outgoing, 'view', split_axis=0, concat_axis=0, tiled=True)  6.54 us
    ppermute x2, starting transfers between devices, passed_along(): return lax.ppermute(x, axis, pairs)  5.48 us
    reshape x4, local copies, waits for them, and re-layouts, banded_second(): bands = [jnp.pad(moved, ((0, 0), (0, 0), (0, 0), (2 * g, rows_n + 2 - tap...  5 us
    ppermute x2, waiting for transfers between devices, passed_along(): return lax.ppermute(x, axis, pairs)  2.32 us
  transfers between devices with their start and end apart: 3, of which 2 were waited for; matrix products, arithmetic and copies ran while one was open for 16% of the time, Pallas kernels for 5%

profile of v4, /device:TPU:15, one launch (start us, length us, event | category | flops | bytes accessed | tf_op | source)
XLA Modules:
  0.0 75.3 jit_solution(2551582473646662077)
XLA Ops:
  0.0 0.0 copy-start
  0.0 0.9 %reshape.176 = s32[16]{0:T(128)S(1)} reshape(s32[1,4,4]{2,1,0:T(4,128)} %param.11) | data formatting | bytes 128 | tf_op jit(solution)/shard_map/reshape | solution.py:314
  0.9 0.2 convert_reduce_fusion
  1.1 0.1 select_reduce_fusion
  1.2 0.1 sub.15
  1.3 7.3 %ask.1 = s32[16,8,128]{2,1,0:T(8,128)S(1)} custom-call(s32[16,8,128]{2,1,0:T(8,128)S(1)} %broadcast_in_dim.27.wanted_ref), custom_call_target="tpu_custom_call" | custom-call | tf_op jit(solution)/shard_map/ask/pallas_call | solution.py:86
  8.7 0.1 reshape.188
  8.8 0.0 copy-done
  8.8 1.9 %gather_fusion = bf16[32,2,32,384]{3,2,1,0:T(8,128)(2,1)} fusion(bf16[32,2,32,384]{3,2,1,0:T(8,128)(2,1)S(1)} %copy-done, s32[1024]{0:T(1024)S(1)} %pad_clamp_fusion), kind=kCustom, calls=%fused_computation | custom fusion | bytes 3145856 | tf_op jit(solution)/shard_map/gather | solution.py:318
  10.7 0.0 copy-start.10
  10.7 0.0 copy-start.8
  10.7 0.0 copy-start.11
  10.7 0.0 copy-start.6
  10.7 6.5 %all-to-all-start = ((bf16[16,2,2,32,384]{4,3,2,1,0:T(8,128)(2,1)}), bf16[16,2,2,32,384]{4,3,2,1,0:T(8,128)(2,1)S(1)}, u32[]{:S(2)}, u32[]{:S(2)}) async-start(bf16[16,2,2,32,384]{4,3,2,1,0:T(8,128)(2,1)} %bitcast.36), calls=%async_computation | async-start | bytes 3145728 | tf_op jit(solution)/shard_map/all_to_all | solution.py:319
  17.2 0.0 copy-start.1
  17.3 0.7 reduce_sum.21
  18.6 0.0 copy-done.10
  18.6 0.6 broadcast_in_dim.52
  19.2 0.0 copy-done.8
  19.2 0.1 copy.41.disp_ref
  19.3 0.0 copy-done.11
  19.3 0.6 broadcast_in_dim.29
  19.9 0.0 copy-done.6
  20.0 0.7 reshape.178
  20.7 1.8 %fusion.11 = (bf16[16,3,3,10,8]{0,4,3,2,1:T(8,128)(2,1)}, bf16[16,3,3,10,8]{0,4,3,2,1:T(8,128)(2,1)}, bf16[16,3,3,10,8]{0,4,3,2,1:T(8,128)(2,1)}, bf16[16,3,3,10,8]{0,4,3,2,1:T(8,128)(2,1)S(1)}) fusion(bf16[16,3,3,3,8]{0,4,3,2,1:T(8,128)(2,1)} %param.16), kind=kLoop, calls=%fused_computation.34 | loop fusion | bytes 99072 | tf_op jit(solution)/shard_map/jit(_pad)/pad | solution.py:286
  22.5 1.0 %copy.37 = bf16[16,720]{1,0:T(8,128)(2,1)S(1)} copy(bf16[16,720]{0,1:T(8,128)(2,1)} %bitcast.40) | data formatting | bytes 46080 | tf_op jit(solution)/shard_map/reshape | solution.py:288
  23.5 1.6 %copy.40 = bf16[16,720]{1,0:T(8,128)(2,1)} copy(bf16[16,720]{0,1:T(8,128)(2,1)} %bitcast.39) | data formatting | bytes 46080 | tf_op jit(solution)/shard_map/reshape | solution.py:288
  25.1 1.6 %copy.39 = bf16[16,720]{1,0:T(8,128)(2,1)} copy(bf16[16,720]{0,1:T(8,128)(2,1)} %bitcast.38) | data formatting | bytes 46080 | tf_op jit(solution)/shard_map/reshape | solution.py:288
  26.8 0.7 copy.38
  27.5 0.0 copy-start.7
  27.5 0.0 copy-start.9
  27.5 0.7 pad.25.conv_ref
  28.2 0.3 prepare.1
  28.5 0.0 copy-start.2
  28.5 0.8 %copy-done.2 = bf16[384,768]{1,0:T(8,128)(2,1)} copy-done((bf16[384,768]{1,0:T(8,128)(2,1)}, bf16[384,768]{1,0:T(8,128)(2,1)S(1)}, u32[]{:S(2)}) %copy-start.2) | copy-done | bytes 589848
  29.3 0.0 copy-start.4
  29.3 0.7 copy-done.4
  30.0 0.8 %pad_maximum_fusion.w2_ref = bf16[64,720]{1,0:T(8,128)(2,1)S(1)} fusion(bf16[16,720]{1,0:T(8,128)(2,1)} %copy.40, bf16[16,720]{1,0:T(8,128)(2,1)} %copy.39, bf16[16,720]{1,0:T(8,128)(2,1)} %copy.38, bf16[16,720]{1,0:T(8,128)(2,1)S(1)} %copy.37), kind=kLoop, calls=%fused_computation.1 | loop fusion | flops 368640 | bytes 184320 | tf_op jit(solution)/shard_map/concatenate | solution.py:291
  30.8 0.7 fusion.6.slot_ref
  31.5 21.9 %all-to-all-done = bf16[16,2,2,32,384]{4,3,2,1,0:T(8,128)(2,1)S(1)} async-done(((bf16[16,2,2,32,384]{4,3,2,1,0:T(8,128)(2,1)}), bf16[16,2,2,32,384]{4,3,2,1,0:T(8,128)(2,1)S(1)}, u32[]{:S(2)}, u32[]{:S(2)}) %all-to-all-start) | async-done | bytes 1572896 | tf_op jit(solution)/shard_map/all_to_all | solution.py:319
  53.4 0.0 copy-done.1
  53.4 3.5 %variance3.1 = (bf16[8,64,384]{2,1,0:T(8,128)(2,1)}, bf16[8,32,384]{2,1,0:T(8,128)(2,1)}) custom-call(s32[4,4]{1,0:T(4,128)S(1)} %fusion.6.slot_ref, s32[8,4]{1,0:T(8,128)S(1)} %copy.41.disp_ref, s32[1]{0:T(128)S(6)} %copy.51.count_ref, bf16[32,64,384]{2,1,0:T(8,128)(2,1)S(1)} %bitcast.32, bf16[256,384]{1,0:T(8,128)(2,1)S(1)} %bitcast.34), custom_call_target="tpu_custom_call" | custom-call | flops 11796480 | bytes 1179648 | tf_op jit(solution)/shard_map/variance3/pallas_call | solution.py:153
  57.0 3.6 %collective-permute-start = (bf16[8,64,384]{2,1,0:T(8,128)(2,1)}, bf16[8,64,384]{2,1,0:T(8,128)(2,1)}, u32[]{:S(2)}, u32[]{:S(2)}) collective-permute-start(bf16[8,64,384]{2,1,0:T(8,128)(2,1)} %get-tuple-element.18.low_ref), channel_id=1, source_target_pairs={{0,1},{1,2},{2,3},{3,4},{4,5},{5,6},{6,7},{7,8},{8,9},{9,10},{10,1... | collective-permute-start | bytes 1179656 | tf_op jit(solution)/shard_map/ppermute | solution.py:14
  60.5 1.9 %collective-permute-start.1 = (bf16[8,32,384]{2,1,0:T(8,128)(2,1)}, bf16[8,32,384]{2,1,0:T(8,128)(2,1)}, u32[]{:S(2)}, u32[]{:S(2)}) collective-permute-start(bf16[8,32,384]{2,1,0:T(8,128)(2,1)} %get-tuple-element.19.top_ref), channel_id=1, source_target_pairs={{1,0},{2,1},{3,2},{4,3},{5,4},{6,5},{7,6},{8,7},{9,8},{10,9},{11,1... | collective-permute-start | bytes 589832 | tf_op jit(solution)/shard_map/ppermute | solution.py:14
  62.5 0.0 copy-done.7
  62.5 0.1 copy.44.b2_ref
  62.6 0.0 copy-done.9
  62.6 0.1 copy.43.b1_ref
  62.7 0.0 copy-start.3
  62.7 0.0 copy-start.5
  62.7 3.7 %variance5.1.mid_ref = bf16[8,160,384]{2,1,0:T(8,128)(2,1)S(1)} custom-call(s32[4,4]{1,0:T(4,128)S(1)} %fusion.6.slot_ref, s32[8,4]{1,0:T(8,128)S(1)} %copy.41.disp_ref, s32[1]{0:T(128)S(6)} %copy.51.count_ref, bf16[32,64,384]{2,1,0:T(8,128)(2,1)S(1)} %bitcast.33, bf16[256,384]{1,0:T(8,128)(2,1)S(1)} %bitcast.35), custom_call_target="tpu_custom_call" | custom-call | flops 19660800 | bytes 1966080 | tf_op jit(solution)/shard_map/variance5/pallas_call | solution.py:153
  66.4 2.3 %collective-permute-done.1.below_ref = bf16[8,32,384]{2,1,0:T(8,128)(2,1)} collective-permute-done((bf16[8,32,384]{2,1,0:T(8,128)(2,1)}, bf16[8,32,384]{2,1,0:T(8,128)(2,1)}, u32[]{:S(2)}, u32[]{:S(2)}) %collective-permute-start.1) | collective-permute-done | bytes 196640 | tf_op jit(solution)/shard_map/ppermute | solution.py:14
  68.7 0.0 collective-permute-done.above_ref
  68.7 0.0 copy-done.3
  68.7 0.0 copy-done.5
  68.7 6.6 %convolutions.1 = f32[4,4,16,192]{3,2,1,0:T(8,128)} custom-call(s32[1]{0:T(128)} %bitcast.first_strip_ref, bf16[8,64,384]{2,1,0:T(8,128)(2,1)} %collective-permute-done.above_ref, bf16[8,32,384]{2,1,0:T(8,128)(2,1)} %get-tuple-element.19.top_ref, bf16[8,160,384]{2,1,0:T(8,128)(2,1)S(1)} %variance5.1.mid_ref, bf16[8,64,384]{2,1,0:T(8,128)(2,1)} %get-tuple-element.18.low_ref, ...), custom_call_target="tpu_custom_call" | custom-call | tf_op jit(solution)/shard_map/convolutions/pallas_call | solution.py:341
  (11 shorter events, 0.1 us)
Async XLA Ops:
  0.0 8.8 %copy-start = (bf16[32,2,32,384]{3,2,1,0:T(8,128)(2,1)S(1)}, bf16[32,2,32,384]{3,2,1,0:T(8,128)(2,1)}, u32[]{:S(2)}) copy-start(bf16[32,2,32,384]{3,2,1,0:T(8,128)(2,1)} %param.10) | copy-start | bytes 4718596
  10.7 7.9 %copy-start.10 = (f32[16]{0:T(128)S(1)}, f32[16]{0:T(128)}, u32[]{:S(2)}) copy-start(f32[16]{0:T(128)} %param.17) | copy-start | bytes 196
  10.7 8.5 %copy-start.8 = (s32[8,4]{0,1:T(4,128)S(1)}, s32[8,4]{0,1:T(4,128)}, u32[]{:S(2)}) copy-start(s32[8,4]{0,1:T(4,128)} %param.13) | copy-start | bytes 388
  10.7 8.6 %copy-start.11 = (f32[8]{0:T(128)S(1)}, f32[8]{0:T(128)}, u32[]{:S(2)}) copy-start(f32[8]{0:T(128)} %param.15) | copy-start | bytes 100
  10.7 9.2 %copy-start.6 = (bf16[3,3,8,3,32]{4,2,3,1,0:T(8,128)(2,1)S(1)}, bf16[3,3,8,3,32]{4,2,3,1,0:T(8,128)(2,1)}, u32[]{:S(2)}) copy-start(bf16[3,3,8,3,32]{4,2,3,1,0:T(8,128)(2,1)} %param.14) | copy-start | bytes 41476
  10.7 42.7 %all-to-all-start = ((bf16[16,2,2,32,384]{4,3,2,1,0:T(8,128)(2,1)}), bf16[16,2,2,32,384]{4,3,2,1,0:T(8,128)(2,1)S(1)}, u32[]{:S(2)}, u32[]{:S(2)}) async-start(bf16[16,2,2,32,384]{4,3,2,1,0:T(8,128)(2,1)} %bitcast.36), calls=%async_computation | async-start | bytes 3145728 | tf_op jit(solution)/shard_map/all_to_all | solution.py:319
  17.2 36.2 %copy-start.1 = (bf16[8,32,384]{2,1,0:T(8,128)(2,1)S(1)}, bf16[8,32,384]{2,1,0:T(8,128)(2,1)}, u32[]{:S(2)}) copy-start(bf16[8,32,384]{2,1,0:T(8,128)(2,1)} %param.9) | copy-start | bytes 589828
  27.5 35.0 %copy-start.7 = (f32[64,1]{0,1:T(1,128)S(1)}, f32[64,1]{0,1:T(1,128)}, u32[]{:S(2)}) copy-start(f32[64,1]{0,1:T(1,128)} %broadcast_in_dim.52) | copy-start | bytes 772
  27.5 35.1 %copy-start.9 = (f32[80,1]{0,1:T(1,128)S(1)}, f32[80,1]{0,1:T(1,128)}, u32[]{:S(2)}) copy-start(f32[80,1]{0,1:T(1,128)} %broadcast_in_dim.29) | copy-start | bytes 964
  28.5 0.8 %copy-start.2 = (bf16[384,768]{1,0:T(8,128)(2,1)}, bf16[384,768]{1,0:T(8,128)(2,1)S(1)}, u32[]{:S(2)}) copy-start(bf16[384,768]{1,0:T(8,128)(2,1)S(1)} %get-tuple-element.24.pick_ref) | copy-start | bytes 1769476
  29.3 0.7 copy-start.4
  57.0 11.8 %collective-permute-start = (bf16[8,64,384]{2,1,0:T(8,128)(2,1)}, bf16[8,64,384]{2,1,0:T(8,128)(2,1)}, u32[]{:S(2)}, u32[]{:S(2)}) collective-permute-start(bf16[8,64,384]{2,1,0:T(8,128)(2,1)} %get-tuple-element.18.low_ref), channel_id=1, source_target_pairs={{0,1},{1,2},{2,3},{3,4},{4,5},{5,6},{6,7},{7,8},{8,9},{9,10},{10,1... | collective-permute-start | bytes 1179656 | tf_op jit(solution)/shard_map/ppermute | solution.py:14
  60.5 8.2 %collective-permute-start.1 = (bf16[8,32,384]{2,1,0:T(8,128)(2,1)}, bf16[8,32,384]{2,1,0:T(8,128)(2,1)}, u32[]{:S(2)}, u32[]{:S(2)}) collective-permute-start(bf16[8,32,384]{2,1,0:T(8,128)(2,1)} %get-tuple-element.19.top_ref), channel_id=1, source_target_pairs={{1,0},{2,1},{3,2},{4,3},{5,4},{6,5},{7,6},{8,7},{9,8},{10,9},{11,1... | collective-permute-start | bytes 589832 | tf_op jit(solution)/shard_map/ppermute | solution.py:14
  62.7 6.1 %copy-start.3 = (bf16[384,768]{1,0:T(8,128)(2,1)S(1)}, bf16[384,768]{1,0:T(8,128)(2,1)}, u32[]{:S(2)}) copy-start(bf16[384,768]{1,0:T(8,128)(2,1)} %copy-done.2) | copy-start | bytes 1769476
  62.7 6.1 %copy-start.5 = (bf16[360,224]{1,0:T(8,128)(2,1)S(1)}, bf16[360,224]{1,0:T(8,128)(2,1)}, u32[]{:S(2)}) copy-start(bf16[360,224]{1,0:T(8,128)(2,1)} %copy-done.4) | copy-start | bytes 483844
